TPU v7x, 128 devices: a whole 4x4x4 slice. The times are simulated.
128 devices in a mesh: dp: 32 (over z, x, core), mp: 4 (over y).
Axes of the slice: x: 4, y: 4, z: 4, core: 2. Of those that a mesh axis runs over, the one named last changes fastest.
Arguments:
- features: bfloat16 [4096, 32, 512], P(('dp', 'mp')), may hold values from -6 to 6
- lengths: int32 [4096], P(('dp', 'mp')), may hold values from 1 to 7, as said below
- dests: int32 [4096], P(('dp', 'mp')), may hold values from 0 to 31, as said below
- offsets: int32 [4096], P(('dp', 'mp')), may hold values from 0 to 511, as said below
- conv_weight: bfloat16 [2, 1024, 512], replicated, may hold values from -0.1875 to 0.1875
- norm_gain: float32 [2, 512], replicated, may hold values from 0.1 to 1.9
- norm_shift: float32 [2, 512], replicated, may hold values from -3 to 3
- proj_weight: bfloat16 [512, 1280], P(None, 'mp'), may hold values from -0.25 to 0.25
- grad_packed: bfloat16 [16384, 1280], P('dp', 'mp'), may hold values from -6 to 6
Outputs:
- packed: bfloat16 [16384, 1280], P('dp', 'mp')
- grad_features: bfloat16 [4096, 32, 512], P(('dp', 'mp'))
- grad_conv: float32 [2, 1024, 512], P(None, ('dp', 'mp'))
- grad_norm: float32 [2, 1024], P(None, ('dp', 'mp'))
- grad_proj: float32 [512, 1280], P('dp', 'mp')
Inputs may be any that keep to these rules, and one draw needn't show every extreme that they name: Utterances 2k and 2k+1 of each device form a pair whose lengths sum to 8. `dests`: both utterances of a pair name the same shard; the 16 pairs of one device name different shards, and every shard is named by exactly 64 pairs. A pair fills one aligned block of 8 rows of its shard that no other pair uses: the first utterance starts at offsets[2k], a multiple of 8, and the second at offsets[2k] + lengths[2k].
All inputs are finite; a program needn't handle non-finite values.
Results may differ from a plain program's by a relative error of at most 0.015.
Values may be sent and summed in bfloat16 or wider, within the bound.
A program may use at most 64 MiB of HBM per device.

v0:
```python
import jax
import jax.numpy as jnp
from jax import lax
from jax.sharding import PartitionSpec as P

epsilon = 1e-05


def norm_gelu(pre_norm, gain_row, shift_row):
    average = jnp.mean(pre_norm, axis=-1, keepdims=True)
    centred = pre_norm - average
    spread = jnp.mean(centred * centred, axis=-1, keepdims=True)
    return jax.nn.gelu(
        centred * lax.rsqrt(spread + epsilon) * gain_row + shift_row, approximate=False
    )


def encode(inputs, conv_weight, norm_gain, norm_shift):
    channels = inputs.shape[-1]
    first_in = inputs.reshape(-1, 2 * channels)
    first_out = jnp.dot(first_in, conv_weight[0], preferred_element_type=jnp.float32)
    hidden, pull_first = jax.vjp(norm_gelu, first_out, norm_gain[0], norm_shift[0])
    hidden = hidden.astype(jnp.bfloat16)
    second_in = hidden.reshape(-1, 2 * channels)
    second = jnp.dot(second_in, conv_weight[1], preferred_element_type=jnp.float32)
    frames, pull_second = jax.vjp(norm_gelu, second, norm_gain[1], norm_shift[1])
    return (frames.astype(jnp.bfloat16), (first_in, second_in, pull_first, pull_second))


def encode_back(grad_frames, kept_state, conv_weight):
    first_in, second_in, pull_first, pull_second = kept_state
    channels = conv_weight.shape[2]
    grad_second, gain_second, shift_second = pull_second(
        lax.optimization_barrier(grad_frames).astype(jnp.float32)
    )
    grad_second = grad_second.astype(jnp.bfloat16)
    grad_hidden = jnp.dot(grad_second, conv_weight[1].T, preferred_element_type=jnp.float32).astype(
        jnp.bfloat16
    )
    grad_hidden = lax.optimization_barrier(grad_hidden).reshape(-1, channels).astype(jnp.float32)
    grad_first, gain_first, shift_first = pull_first(grad_hidden)
    grad_first = grad_first.astype(jnp.bfloat16)
    grad_inputs = jnp.dot(grad_first, conv_weight[0].T, preferred_element_type=jnp.float32).astype(
        jnp.bfloat16
    )
    grad_weight = jnp.stack(
        [
            jnp.dot(first_in.T, grad_first, preferred_element_type=jnp.float32),
            jnp.dot(second_in.T, grad_second, preferred_element_type=jnp.float32),
        ]
    )
    grad_norms = jnp.stack(
        [jnp.concatenate([gain_first, shift_first]), jnp.concatenate([gain_second, shift_second])]
    )
    return (grad_inputs, grad_weight, grad_norms)


def local(
    features, lengths, dests, offsets, conv_weight, norm_gain, norm_shift, proj_weight, grad_packed
):
    utt_count, positions, channels = features.shape
    frame_count = positions // 4
    pair_count = utt_count // 2
    dp_count = lax.axis_size("dp")
    mp_count = lax.axis_size("mp")
    block_count = pair_count * mp_count
    first_len = lengths[0::2]
    pair_dest = dests[0::2]
    pair_block = offsets[0::2] // frame_count
    slot_frames, kept_state = encode(
        features.reshape(-1, channels), conv_weight, norm_gain, norm_shift
    )
    slot_frames = slot_frames.reshape(pair_count, 2 * frame_count, channels)
    frame_ids = jnp.arange(frame_count, dtype=jnp.int32)[None, :]
    source_frame = jnp.where(
        frame_ids < first_len[:, None], frame_ids, frame_count + frame_ids - first_len[:, None]
    )
    pair_frames = jnp.take_along_axis(slot_frames, source_frame[:, :, None], axis=1)
    send_index = jnp.full((dp_count,), block_count, jnp.int32).at[pair_dest].set(pair_block)
    send_index_all = jnp.broadcast_to(send_index[:, None], (dp_count, mp_count)).reshape(-1)
    send_frames = (
        jnp.zeros((dp_count, frame_count, channels), jnp.bfloat16).at[pair_dest].set(pair_frames)
    )
    send_frames = jnp.broadcast_to(
        send_frames[:, None], (dp_count, mp_count, frame_count, channels)
    )
    send_frames = send_frames.reshape(dp_count * mp_count, frame_count, channels)
    got_frames, got_index = (
        lax.all_to_all(send_frames, ("dp", "mp"), split_axis=0, concat_axis=0, tiled=True),
        lax.all_to_all(send_index_all, ("dp", "mp"), split_axis=0, concat_axis=0, tiled=True),
    )
    packed_in = jnp.zeros((block_count, frame_count, channels), jnp.bfloat16)
    packed_in = packed_in.at[got_index].set(got_frames, mode="drop").reshape(-1, channels)
    packed = jnp.dot(packed_in, proj_weight, preferred_element_type=jnp.float32).astype(
        jnp.bfloat16
    )
    grad_proj = lax.psum_scatter(
        jnp.dot(packed_in.T, grad_packed, preferred_element_type=jnp.float32).astype(jnp.bfloat16),
        "dp",
        scatter_dimension=0,
        tiled=True,
    ).astype(jnp.float32)
    grad_rows = jnp.dot(grad_packed, proj_weight.T, preferred_element_type=jnp.float32)
    grad_rows = grad_rows.reshape(block_count, frame_count, channels)
    partial_sums = jnp.take(grad_rows, got_index, axis=0, mode="fill", fill_value=0.0)
    returned = lax.all_to_all(partial_sums, ("dp", "mp"), split_axis=0, concat_axis=0, tiled=True)
    returned = returned.reshape(dp_count, mp_count, frame_count, channels)
    grad_blocks = jnp.sum(returned, axis=1).astype(jnp.bfloat16)
    grad_pair = grad_blocks[pair_dest]
    all_ids = jnp.arange(2 * frame_count, dtype=jnp.int32)[None, :]
    in_first = all_ids < frame_count
    from_frame = jnp.where(in_first, all_ids, all_ids - frame_count + first_len[:, None])
    is_valid = jnp.where(
        in_first,
        all_ids < first_len[:, None],
        all_ids - frame_count < frame_count - first_len[:, None],
    )
    gathered = jnp.take_along_axis(
        grad_pair, jnp.minimum(from_frame, frame_count - 1)[:, :, None], axis=1
    )
    grad_slots = jnp.where(is_valid[:, :, None], gathered, jnp.zeros_like(gathered)).reshape(
        -1, channels
    )
    grad_input, grad_weight, grad_norms = encode_back(grad_slots, kept_state, conv_weight)
    grad_features = grad_input.reshape(utt_count, positions, channels)
    grad_conv, grad_norm = (
        lax.psum_scatter(grad_weight, ("dp", "mp"), scatter_dimension=1, tiled=True),
        lax.psum_scatter(grad_norms, ("dp", "mp"), scatter_dimension=1, tiled=True),
    )
    return (packed, grad_features, grad_conv, grad_norm, grad_proj)


def solution(mesh):
    return jax.shard_map(
        local,
        mesh=mesh,
        in_specs=(
            P(("dp", "mp"), None, None),
            P(("dp", "mp")),
            P(("dp", "mp")),
            P(("dp", "mp")),
            P(),
            P(),
            P(),
            P(None, "mp"),
            P("dp", "mp"),
        ),
        out_specs=(
            P("dp", "mp"),
            P(("dp", "mp"), None, None),
            P(None, ("dp", "mp"), None),
            P(None, ("dp", "mp")),
            P("dp", "mp"),
        ),
        check_vma=False,
    )
```

profile of v0, /device:TPU:1, one launch (start us, length us, event | category | flops | bytes accessed | tf_op | source)
XLA Modules:
  0.0 301.9 jit_solution(10330396382865330285)
XLA Ops:
  11.6 11.5 %all-to-all-start = ((s32[128,1,1]{2,1,0:T(1,128)}), s32[128,1,1]{2,1,0:T(1,128)S(1)}, u32[]{:S(2)}, u32[]{:S(2)}) async-start(s32[128,1,1]{2,1,0:T(1,128)} %all_to_all.22), calls=%async_computation | async-start | bytes 131072 | tf_op jit(solution)/shard_map/all_to_all | solution.py:90
  23.1 1.4 reshape_reshape.3
  24.6 2.4 fusion.51
  29.1 3.8 %multiply_convert_fusion = (bf16[512,512]{0,1:T(8,128)(2,1)S(1)}, f32[512,512]{0,1:T(8,128)}) fusion(f32[512,512]{0,1:T(8,128)S(1)} %get-tuple-element.48, f32[512]{0:T(512)S(1)} %bitcast.64, f32[512]{0:T(512)S(1)} %bitcast.61, f32[512]{0:T(512)S(1)} %fusion.39, f32[512]{0:T(512)S(1)} %broadcast_multiply_fusion), kind=kLoop, calls=%fused_computation.30 | loop fusion | flops 18087936 | bytes 2629632 | tf_op jit(solution)/shard_map/convert_element_type | solution.py:23
  33.9 2.4 reduce
  36.3 2.1 gather_fusion
  38.4 3.1 %broadcast_select_fusion = f32[128,8,512]{2,1,0:T(8,128)} fusion(f32[128,8,512]{2,1,0:T(8,128)} %gather_fusion, pred[128]{0:T(512)(128)(4,1)S(1)} %compare_and_fusion), kind=kLoop, calls=%fused_computation.29 | loop fusion | flops 524288 | bytes 4194432 | tf_op jit(solution)/shard_map/jit(_take)/select_n | solution.py:105
  41.5 10.2 %all-to-all-start.2 = ((f32[128,8,512]{2,1,0:T(8,128)}), f32[128,8,512]{2,1,0:T(8,128)}, u32[]{:S(2)}, u32[]{:S(2)}) async-start(f32[128,8,512]{2,1,0:T(8,128)} %broadcast_select_fusion), calls=%async_computation.2 | async-start | bytes 4194304 | tf_op jit(solution)/shard_map/all_to_all | solution.py:106
  52.8 1.8 fusion.52
  54.9 27.1 %all-to-all-done.2 = f32[128,8,512]{2,1,0:T(8,128)} async-done(((f32[128,8,512]{2,1,0:T(8,128)}), f32[128,8,512]{2,1,0:T(8,128)}, u32[]{:S(2)}, u32[]{:S(2)}) %all-to-all-start.2) | async-done | bytes 2097184 | tf_op jit(solution)/shard_map/all_to_all | solution.py:106
  81.9 1.8 bitcast_reduce_fusion
  84.4 2.0 gather_fusion.3
  86.6 1.6 multiply_reduce_fusion.3
  89.1 1.1 reshape.459
  90.2 2.5 copy.30
  92.8 1.3 gather_fusion.2
  95.3 1.1 broadcast_in_dim.131
  96.4 4.7 %all-to-all-start.1 = ((bf16[128,8,512]{2,1,0:T(8,128)(2,1)}), bf16[128,8,512]{2,1,0:T(8,128)(2,1)}, u32[]{:S(2)}, u32[]{:S(2)}) async-start(bf16[128,8,512]{2,1,0:T(8,128)(2,1)} %bitcast.60), calls=%async_computation.1 | async-start | bytes 2097152 | tf_op jit(solution)/shard_map/all_to_all | solution.py:89
  101.2 2.2 multiply_reduce_fusion
  103.5 1.3 fusion.44
  104.7 15.4 %all-to-all-done.1 = bf16[128,8,512]{2,1,0:T(8,128)(2,1)} async-done(((bf16[128,8,512]{2,1,0:T(8,128)(2,1)}), bf16[128,8,512]{2,1,0:T(8,128)(2,1)}, u32[]{:S(2)}, u32[]{:S(2)}) %all-to-all-start.1) | async-done | bytes 1048608 | tf_op jit(solution)/shard_map/all_to_all | solution.py:89
  120.2 9.7 %scatter_fusion.1 = bf16[64,8,512]{2,1,0:T(8,128)(2,1)S(1)} fusion(bf16[64,8,512]{2,1,0:T(8,128)(2,1)S(1)} %broadcast_in_dim.124, s32[128]{0:T(128)S(1)} %fusion.41, bf16[128,8,512]{2,1,0:T(8,128)(2,1)} %all-to-all-done.1), kind=kCustom, calls=%fused_computation.6 | custom fusion | bytes 3146240 | tf_op jit(solution)/shard_map/scatter | solution.py:93
  130.0 1.3 convolution_convert_fusion.2
  132.2 1.9 convolution_bitcast_fusion
  134.1 2.3 pad_maximum_fusion
  136.4 7.3 %copy.33 = f32[2,1024,512]{2,0,1:T(2,128)} copy(f32[2,1024,512]{1,2,0:T(8,128)} %pad_maximum_fusion) | data formatting | bytes 8388608 | tf_op jit(solution)/shard_map/stack | solution.py:46
  143.7 1.2 copy-done.4
  144.9 2.0 convolution_convert_fusion
  146.9 1.2 reshape.458
  148.1 63.6 %all-reduce.1 = f32[2,1024]{1,0:T(2,128)S(1)} all-reduce(f32[2,1024]{1,0:T(2,128)S(1)} %pad_maximum_fusion.1), channel_id=3, replica_groups=mesh['dp'=32,'mp'=4] {'dp','mp'}, use_global_device_ids=true, to_apply=%region_17.18.clone | all-reduce | flops 2048 | bytes 16384
  213.5 1.3 convert_element_type.51
  214.8 78.2 %all-reduce.4.cloned.1.call-done = f32[2,1024,512]{2,0,1:T(2,128)} async-done(((f32[2,1024,512]{2,0,1:T(2,128)}), f32[2,1024,512]{2,0,1:T(2,128)}) %all-reduce.4.cloned.1.call-update) | async-done | bytes 4194320
  (133 shorter events, 14.8 us)
Async XLA Ops:
  8.0 24.9 %copy-start = (bf16[512,320]{0,1:T(8,128)(2,1)S(1)}, bf16[512,320]{0,1:T(8,128)(2,1)}, u32[]{:S(2)}) copy-start(bf16[512,320]{0,1:T(8,128)(2,1)} %param.17) | copy-start | bytes 983044
  11.6 22.4 %all-to-all-start = ((s32[128,1,1]{2,1,0:T(1,128)}), s32[128,1,1]{2,1,0:T(1,128)S(1)}, u32[]{:S(2)}, u32[]{:S(2)}) async-start(s32[128,1,1]{2,1,0:T(1,128)} %all_to_all.22), calls=%async_computation | async-start | bytes 131072 | tf_op jit(solution)/shard_map/all_to_all | solution.py:90
  23.1 9.7 %copy-start.26 = (s32[16]{0:T(128)}, s32[16]{0:T(128)S(1)}, u32[]{:S(2)}) copy-start(s32[16]{0:T(128)S(1)} %iota_add_fusion) | copy-start | bytes 196
  23.1 9.7 %copy-start.24 = (pred[16]{0:T(512)(128)(4,1)}, pred[16]{0:T(512)(128)(4,1)S(1)}, u32[]{:S(2)}) copy-start(pred[16]{0:T(512)(128)(4,1)S(1)} %iota_compare_fusion.2) | copy-start | bytes 52
  24.5 2.6 copy-start.2
  24.5 3.2 %copy-start.28 = (f32[2,512]{1,0:T(2,128)S(1)}, f32[2,512]{1,0:T(2,128)}, u32[]{:S(2)}) copy-start(f32[2,512]{1,0:T(2,128)} %param.14) | copy-start | bytes 12292
  24.6 3.8 %copy-start.29 = (f32[2,512]{1,0:T(2,128)S(1)}, f32[2,512]{1,0:T(2,128)}, u32[]{:S(2)}) copy-start(f32[2,512]{1,0:T(2,128)} %param.15) | copy-start | bytes 12292
  24.6 4.4 %copy-start.30 = (s32[32]{0:T(128)S(1)}, s32[32]{0:T(128)}, u32[]{:S(2)}) copy-start(s32[32]{0:T(128)} %param.10) | copy-start | bytes 388
  27.0 6.0 %copy-start.7 = (bf16[512,320]{0,1:T(8,128)(2,1)S(1)}, bf16[512,320]{0,1:T(8,128)(2,1)}, u32[]{:S(2)}) copy-start(bf16[512,320]{0,1:T(8,128)(2,1)} %param.16) | copy-start | bytes 983044
  27.8 5.0 %copy-start.10 = (f32[512]{0:T(512)}, f32[512]{0:T(512)S(1)}, u32[]{:S(2)}) copy-start(f32[512]{0:T(512)S(1)} %fusion.39) | copy-start | bytes 6148
  28.4 5.0 %copy-start.12 = (f32[1,512]{1,0:T(1,128)}, f32[1,512]{1,0:T(1,128)S(1)}, u32[]{:S(2)}) copy-start(f32[1,512]{1,0:T(1,128)S(1)} %get-tuple-element.44) | copy-start | bytes 6148
  29.0 4.5 %copy-start.14 = (f32[1,512]{1,0:T(1,128)}, f32[1,512]{1,0:T(1,128)S(1)}, u32[]{:S(2)}) copy-start(f32[1,512]{1,0:T(1,128)S(1)} %get-tuple-element.42) | copy-start | bytes 6148
  29.1 4.4 %copy-start.20 = (s32[16]{0:T(128)}, s32[16]{0:T(128)S(1)}, u32[]{:S(2)}) copy-start(s32[16]{0:T(128)S(1)} %slice.31) | copy-start | bytes 196
  33.8 18.9 %copy-start.5 = (bf16[256,1024]{1,0:T(8,128)(2,1)}, bf16[256,1024]{1,0:T(8,128)(2,1)S(1)}, u32[]{:S(2)}) copy-start(bf16[256,1024]{1,0:T(8,128)(2,1)S(1)} %reshape.452) | copy-start | bytes 1572868
  41.5 10.3 %copy-start.21 = (s32[16]{0:T(128)S(1)}, s32[16]{0:T(128)}, u32[]{:S(2)}) copy-start(s32[16]{0:T(128)} %copy-done.20) | copy-start | bytes 196
  41.5 10.6 %copy-start.27 = (s32[16]{0:T(128)S(1)}, s32[16]{0:T(128)}, u32[]{:S(2)}) copy-start(s32[16]{0:T(128)} %copy-done.26) | copy-start | bytes 196
  41.5 10.8 %copy-start.25 = (pred[16]{0:T(512)(128)(4,1)S(1)}, pred[16]{0:T(512)(128)(4,1)}, u32[]{:S(2)}) copy-start(pred[16]{0:T(512)(128)(4,1)} %copy-done.24) | copy-start | bytes 52
  41.5 11.2 %copy-start.23 = (s32[16]{0:T(128)S(1)}, s32[16]{0:T(128)}, u32[]{:S(2)}) copy-start(s32[16]{0:T(128)} %copy-done.22) | copy-start | bytes 196
  41.5 40.4 %all-to-all-start.2 = ((f32[128,8,512]{2,1,0:T(8,128)}), f32[128,8,512]{2,1,0:T(8,128)}, u32[]{:S(2)}, u32[]{:S(2)}) async-start(f32[128,8,512]{2,1,0:T(8,128)} %broadcast_select_fusion), calls=%async_computation.2 | async-start | bytes 4194304 | tf_op jit(solution)/shard_map/all_to_all | solution.py:106
  83.8 2.8 copy-start.18
  83.8 2.8 copy-start.19
  94.2 7.0 %copy-start.1 = (f32[512,512]{0,1:T(8,128)S(1)}, f32[512,512]{0,1:T(8,128)}, u32[]{:S(2)}) copy-start(f32[512,512]{0,1:T(8,128)} %get-tuple-element.39) | copy-start | bytes 3145732
  94.2 7.0 %copy-start.11 = (f32[512]{0:T(512)S(1)}, f32[512]{0:T(512)}, u32[]{:S(2)}) copy-start(f32[512]{0:T(512)} %copy-done.10) | copy-start | bytes 6148
  94.2 7.0 %copy-start.13 = (f32[1,512]{1,0:T(1,128)S(1)}, f32[1,512]{1,0:T(1,128)}, u32[]{:S(2)}) copy-start(f32[1,512]{1,0:T(1,128)} %copy-done.12) | copy-start | bytes 6148
  94.2 7.0 %copy-start.15 = (f32[1,512]{1,0:T(1,128)S(1)}, f32[1,512]{1,0:T(1,128)}, u32[]{:S(2)}) copy-start(f32[1,512]{1,0:T(1,128)} %copy-done.14) | copy-start | bytes 6148
  96.4 23.8 %all-to-all-start.1 = ((bf16[128,8,512]{2,1,0:T(8,128)(2,1)}), bf16[128,8,512]{2,1,0:T(8,128)(2,1)}, u32[]{:S(2)}, u32[]{:S(2)}) async-start(bf16[128,8,512]{2,1,0:T(8,128)(2,1)} %bitcast.60), calls=%async_computation.1 | async-start | bytes 2097152 | tf_op jit(solution)/shard_map/all_to_all | solution.py:89
  101.1 112.4 %reduce-scatter.3.cloned.1.call-start = ((), (), s32[]{:S(2)}) async-start(), calls=%async_computation.4 | async-start | bytes 405504 | tf_op jit(solution)/shard_map/reduce_scatter | solution.py:97
  101.2 2.2 copy-start.17
  120.2 11.3 %copy-start.6 = (bf16[256,1024]{1,0:T(8,128)(2,1)S(1)}, bf16[256,1024]{1,0:T(8,128)(2,1)}, u32[]{:S(2)}) copy-start(bf16[256,1024]{1,0:T(8,128)(2,1)} %copy-done.5) | copy-start | bytes 1572868
  130.0 2.2 copy-start.3
  131.3 161.7 %all-reduce.4.cloned.1.call-start = ((), (), s32[]{:S(2)}) async-start(), calls=%async_computation.5 | async-start | bytes 8388608
  144.9 67.5 %copy-start.8 = (bf16[512,320]{0,1:T(8,128)(2,1)S(1)}, bf16[512,320]{0,1:T(8,128)(2,1)}, u32[]{:S(2)}) copy-start(bf16[512,320]{0,1:T(8,128)(2,1)} %param.16) | copy-start | bytes 983044
  (4 other events, 4.4 us)
Sparse Core Ops, SparseCore 0:
  131.4 67.5 reduce-scatter.2
Sparse Core Ops, SparseCore 1:
  143.8 149.2 all-reduce.3
where the time goes:
time: 303 us; the launch traced here: 302 us
  waiting for transfers between devices  121 us (40%)
  blocking collectives  63.6 us (21%)
  local copies, waits for them, and re-layouts  41.5 us (14%)
  starting transfers between devices  26.7 us (9%)
  other arithmetic  21.1 us (7%)
  between operations  16.1 us (5%)
  matrix products  12 us (4%)
    unnamed x3, waiting for transfers between devices  78.3 us
    unnamed x1, blocking collectives  63.6 us
    all_to_all x1, waiting for transfers between devices, local(): lax.all_to_all(partial_sums, ('dp', 'mp'), split_axis=0, concat_axis=0, t...  27.1 us
    all_to_all x1, waiting for transfers between devices, local(): lax.all_to_all(send_frames, ('dp', 'mp'), split_axis=0, concat_axis=0, ti...  15.4 us
    all_to_all x1, starting transfers between devices, local(): lax.all_to_all(send_index_all, ('dp', 'mp'), split_axis=0, concat_axis=0,...  11.5 us
    all_to_all x1, starting transfers between devices, local(): lax.all_to_all(partial_sums, ('dp', 'mp'), split_axis=0, concat_axis=0, t...  10.2 us
    scatter x1, local copies, waits for them, and re-layouts, local(): packed_in.at[got_index].set(got_frames, mode='drop').reshape(-1, channels)  9.74 us
    another operation x1, local copies, waits for them, and re-layouts, encode_back(): jnp.stack([jnp.dot(first_in.T, grad_first, preferred_element_type=jnp.flo...  7.28 us
  transfers between devices with their start and end apart: 5, of which 3 were waited for; matrix products, arithmetic and copies ran while one was open for 12% of the time, Pallas kernels for 0%

commit v1 on v0

v1 whole, which is shorter than its diff:
```python
import jax
import jax.numpy as jnp
from jax import lax
from jax.experimental import pallas as pl
from jax.experimental.pallas import tpu as pltpu
from jax.sharding import PartitionSpec as P

EPSILON = 1e-05
BF = jnp.bfloat16
F32 = jnp.float32
MESH = pl.DeviceIdType.MESH
NN = (((1,), (0,)), ((), ()))
NT = (((1,), (1,)), ((), ()))
TN = (((0,), (0,)), ((), ()))
LANE = 128


def dot(a, b, dims=NN):
    return lax.dot_general(a, b, dims, preferred_element_type=F32)


def iota(shape, dim):
    return lax.broadcasted_iota(jnp.int32, shape, dim)


def kernel(
    idx_ref, tgt_ref, gain_ref, shift_ref, feat_hbm, weight_hbm, proj_hbm, gp_hbm,
    packed_out, gfeat_out, gconv_out, gproj_out, gnorm_out,
    xb, wv, gpv, xf, act, pre, xhat0, der0, rstd0, xhat1, der1, rstd1, hid, frm, slots,
    tbl, query, gsend, grecv, psend, precv, pall, packv,
    gh, gf, gx, xo, gfv,
    convp, convr, convb, conv1, convb1, conv2, convb2, conv3,
    projp, projr, projb, proj1, projb1, proj2, projb2, proj3,
    nrm, nrmr, nrm1,
    in_sem, out_sem, idx_s, idx_r, ag_s, ag_r, a2a_s, a2a_r, rs_s, rs_r, nm_s, nm_r,
):
    dp = lax.axis_index("dp")
    y = lax.axis_index("mp")
    z, q = dp // 8, dp % 8
    x, c = q // 2, q % 2
    d = dp * 4 + y

    def dp_of(zz, xx, cc):
        return zz * 8 + xx * 2 + cc

    def remote(src, dst, ssem, rsem, to):
        return pltpu.make_async_remote_copy(
            src_ref=src, dst_ref=dst, send_sem=ssem, recv_sem=rsem, device_id=to, device_id_type=MESH
        )

    def await_bytes(ref, sem):
        pltpu.make_async_copy(ref, ref, sem).wait()

    loads = [
        pltpu.make_async_copy(feat_hbm, xb, in_sem.at[0]),
        pltpu.make_async_copy(weight_hbm, wv, in_sem.at[1]),
        pltpu.make_async_copy(proj_hbm, pall.at[y], in_sem.at[2]),
        pltpu.make_async_copy(gp_hbm, gpv, in_sem.at[3]),
    ]
    for one in (2, 0, 1, 3):
        loads[one].start()

    partners = (
        [(dp, (y + k) % 4) for k in range(1, 4)]
        + [(z * 8 + (q + k) % 8, y) for k in range(1, 8)]
        + [(((z + k) % 4) * 8 + q, y) for k in range(1, 4)]
    )
    barrier = pltpu.get_barrier_semaphore()
    for to in partners:
        pl.semaphore_signal(barrier, inc=1, device_id=to, device_id_type=MESH)
    tbl[z, q, y] = idx_ref[...]
    pl.semaphore_wait(barrier, len(partners))

    sends = []

    def launch(copy):
        copy.start()
        sends.append(copy)

    for k in range(1, 4):
        launch(remote(tbl.at[z, q, y], tbl.at[z, q, y], idx_s.at[k - 1], idx_r.at[0], (dp, (y + k) % 4)))
    loads[2].wait()
    up, down, far = (y + 1) % 4, (y + 3) % 4, (y + 2) % 4
    launch(remote(pall.at[y, c], pall.at[y, c], ag_s.at[0], ag_r.at[0], (dp, up)))
    launch(remote(pall.at[y, c], pall.at[y, c], ag_s.at[1], ag_r.at[1], (dp, down)))

    loads[0].wait()

    @pl.loop(0, 8)
    def _(i):
        rows = xb[pl.ds(pl.multiple_of(i * 128, 128), 128), :].astype(F32)
        for j in range(4):
            xf[j] = rows[:, j * LANE : (j + 1) * LANE]
        for k in range(4):
            part = jnp.concatenate([xf[j, pl.ds(k, 32, stride=4), :] for j in range(4)], axis=1)
            act[pl.ds(pl.multiple_of((k // 2) * 256 + i * 32, 32), 32), (k % 2) * 512 : (k % 2) * 512 + 512] = part.astype(BF)

    await_bytes(tbl.at[z, q, pl.ds(0, 3)], idx_r.at[0])
    for k in range(1, 8):
        launch(remote(tbl.at[z, q], tbl.at[z, q], idx_s.at[2 + k], idx_r.at[1], (z * 8 + (q + k) % 8, y)))

    loads[1].wait()
    pre[...] = dot(act[...], wv[0])

    await_bytes(pall.at[down, c], ag_r.at[0])
    launch(remote(pall.at[down, c, pl.ds(0, 128)], pall.at[down, c, pl.ds(0, 128)], ag_s.at[2], ag_r.at[2], (dp, up)))
    await_bytes(pall.at[up, c], ag_r.at[1])
    launch(remote(pall.at[up, c, pl.ds(128, 128)], pall.at[up, c, pl.ds(128, 128)], ag_s.at[3], ag_r.at[3], (dp, down)))

    await_bytes(tbl.at[z, pl.ds(0, 7)], idx_r.at[1])
    for k in range(1, 4):
        launch(remote(tbl.at[z], tbl.at[z], idx_s.at[9 + k], idx_r.at[2], (((z + k) % 4) * 8 + q, y)))

    def norm_gelu(source, gain, shift, xhat, der, rstd, start, count):
        v = source[pl.ds(start, count), :]
        mean = jnp.mean(v, axis=-1, keepdims=True)
        centred = v - mean
        spread = jnp.mean(centred * centred, axis=-1, keepdims=True)
        inv = lax.rsqrt(spread + EPSILON)
        normal = centred * inv
        arg = normal * gain + shift
        cdf = 0.5 + 0.5 * lax.erf(arg * (2.0**-0.5))
        xhat[pl.ds(start, count), :] = normal
        der[pl.ds(start, count), :] = cdf + arg * (jnp.exp(-0.5 * arg * arg) * 0.3989422804014327)
        rstd[pl.ds(start, count), :] = jnp.broadcast_to(inv, (count, LANE))
        return arg * cdf

    gain0, shift0 = gain_ref[0:1, :], shift_ref[0:1, :]
    gain1, shift1 = gain_ref[1:2, :], shift_ref[1:2, :]

    def first_rows(lo, hi):
        @pl.loop(lo, hi)
        def _(i):
            start = pl.multiple_of(i * 32, 32)
            for h in range(2):
                out = norm_gelu(pre, gain0, shift0, xhat0, der0, rstd0, pl.multiple_of(start + h * 256, 32), 32)
                hid[pl.ds(start, 32), h * 512 : (h + 1) * 512] = out.astype(BF)

    first_rows(0, 4)

    await_bytes(tbl.at[pl.ds(0, 3)], idx_r.at[2])
    table = tbl[...].reshape(128, LANE).astype(BF)
    pick = (iota((128, 512), 0) == dp).astype(F32).astype(BF)
    spread_s = ((iota((1024, 128), 0) >> 3) == iota((1024, 128), 1)).astype(F32).astype(BF)
    wanted = dot(spread_s, dot(table, pick).astype(BF))
    r_id = (iota((1024, 512), 0) & 7).astype(F32)
    c_id = iota((1024, 512), 1).astype(F32)
    one_hot = (wanted * 8.0 + r_id == c_id).astype(F32).astype(BF)
    loads[3].wait()
    gsend[...] = dot(one_hot, gpv[...]).astype(BF).reshape(128, 8, 320)

    own_g = pltpu.make_async_copy(gsend.at[d], grecv.at[y, dp], a2a_r.at[0])
    own_g.start()

    @pl.loop(1, 128)
    def _(k):
        to = (d + k) % 128
        remote(gsend.at[to], grecv.at[y, dp], a2a_s.at[0], a2a_r.at[0], (to // 4, to % 4)).start()

    await_bytes(pall.at[far, c, pl.ds(0, 128)], ag_r.at[2])
    await_bytes(pall.at[far, c, pl.ds(128, 128)], ag_r.at[3])
    mate = (dp_of(z, x, 1 - c), y)
    for n, at in enumerate((up, down, far)):
        launch(remote(pall.at[at, c], pall.at[at, c], ag_s.at[4 + n], ag_r.at[4 + n], mate))

    first_rows(4, 8)
    pre[pl.ds(0, 256), :] = dot(hid[...], wv[1])

    @pl.loop(0, 8)
    def _(i):
        start = pl.multiple_of(i * 32, 32)
        out = norm_gelu(pre, gain1, shift1, xhat1, der1, rstd1, start, 32)
        frm[pl.ds(start, 32), :] = out.astype(BF)

    place = (iota((256, 256), 0) == tgt_ref[...]).astype(F32).astype(BF)
    slots[...] = dot(place, frm[...]).astype(BF)
    for n, at in enumerate((up, down, far)):
        await_bytes(pall.at[at, 1 - c], ag_r.at[4 + n])
    for m in range(4):
        width = pall[m].reshape(512, 320)
        psend[m] = dot(slots[...], width).astype(BF).reshape(32, 8, 320)

    await_bytes(grecv, a2a_r.at[0])
    own_p = pltpu.make_async_copy(psend.at[y, dp], precv.at[d], a2a_r.at[1])
    own_p.start()

    @pl.loop(1, 128)
    def _(k):
        to = (d + k) % 128
        remote(psend.at[to % 4, to // 4], precv.at[d], a2a_s.at[1], a2a_r.at[1], (to // 4, to % 4)).start()

    total = None
    for m in range(4):
        width = pall[m].reshape(512, 320)
        part = dot(grecv[m].reshape(256, 320), width, NT)
        total = part if total is None else total + part
    grad_frames = dot(place, total.astype(BF), TN)
    gh[pl.ds(0, 256), :] = grad_frames

    sizes = dict(x=x, y=y, z=z)

    def peer(axis, k):
        if axis == "x":
            return (dp_of(z, (x + k) % 4, c), y)
        if axis == "z":
            return (dp_of((z + k) % 4, x, c), y)
        return (dp, (y + k) % 4)

    def chunk(ref, lead, dims, axis, at):
        pos = dims.index(axis)
        return ref.at[tuple(lead) + (slice(None),) * pos + (at,)]

    def scatter(source, landing, lead, dims, axis, sem):
        for k in range(1, 4):
            at = (sizes[axis] + k) % 4
            launch(
                remote(
                    chunk(source, lead, dims, axis, at),
                    landing.at[tuple(lead) + (k - 1,)],
                    rs_s.at[sem, k - 1],
                    rs_r.at[sem],
                    peer(axis, k),
                )
            )

    def gather(source, landing, lead, dims, axis, sem):
        await_bytes(landing.at[tuple(lead) + (pl.ds(0, 3),)], rs_r.at[sem])
        total = chunk(source, lead, dims, axis, sizes[axis])[...].astype(F32)
        for k in range(3):
            total = total + landing[tuple(lead) + (k,)].astype(F32)
        return total

    def norm_back(upstream, gain, xhat, der, rstd, start, rows, count, sums):
        dy = upstream * der[pl.ds(start, count), :]
        normal = xhat[pl.ds(start, count), :]
        dyn = dy * normal
        dg = sums[0] + dyn.reshape(count // 8, 8, 512).sum(axis=0)
        ds = sums[1] + dy.reshape(count // 8, 8, 512).sum(axis=0)
        mean_d = jnp.mean(dy * gain, axis=-1, keepdims=True)
        mean_dn = jnp.mean(dyn * gain, axis=-1, keepdims=True)
        inv = rstd[pl.ds(start, count), :][:, 0:1]
        return inv * (dy * gain - mean_d - normal * mean_dn), (dg, ds)

    def put_norm(layer, sums):
        for half in range(2):
            row = sums[half].sum(axis=0, keepdims=True)
            for j in range(4):
                nrm[layer * 8 + half * 4 + j : layer * 8 + half * 4 + j + 1, :] = row[:, j * LANE : (j + 1) * LANE]

    zeros = (jnp.zeros((8, 512), F32), jnp.zeros((8, 512), F32))

    def second_body(i, sums):
        start = pl.multiple_of(i * 32, 32)
        out, sums = norm_back(gh[pl.ds(start, 32), :], gain1, xhat1, der1, rstd1, start, None, 32, sums)
        gf[pl.ds(start, 32), :] = out.astype(BF)
        return sums

    sums1 = lax.fori_loop(0, 8, second_body, zeros)
    put_norm(1, sums1)
    grad_second = gf[pl.ds(0, 256), :]
    for h in range(2):
        gh[pl.ds(h * 256, 256), :] = dot(grad_second, wv[1, pl.ds(h * 512, 512), :], NT).astype(BF).astype(F32)

    for h in range(8):
        part = dot(hid[:, h * 128 : (h + 1) * 128], grad_second, TN).astype(BF)
        for j in range(4):
            convp[1, j, h // 2, (h % 2) * 2 : (h % 2) * 2 + 2] = part[:, j * LANE : (j + 1) * LANE].reshape(2, 2, 4, 8, LANE)
    for j in range(4):
        launch(remote(convp.at[1, j, :, :, 1 - c], convr.at[1, j], rs_s.at[j, 3], rs_r.at[j], mate))

    for m in range(4):
        part = dot(slots[...], grecv[m].reshape(256, 320), TN).astype(BF)
        projp[m] = part.reshape(4, 4, 2, 16, 320)
    for m in range(4):
        launch(remote(projp.at[m, :, :, 1 - c], projr.at[m], rs_s.at[4 + m, 3], rs_r.at[4 + m], mate))

    conv_orders = (("x", "y", "z"), ("y", "z", "x"), ("z", "x", "y"), ("x", "z", "y"))
    proj_orders = (("x", "z"), ("z", "x"), ("x", "z"), ("z", "x"))

    def conv_core(layer, j, sem):
        await_bytes(convr.at[layer, j], rs_r.at[sem])
        convb[layer, j] = (
            convp[layer, j, :, :, c].astype(F32) + convr[layer, j].astype(F32)
        ).astype(BF)

    def without(dims, axis):
        return tuple(one for one in dims if one != axis)

    base = ("z", "x", "y")

    def conv_send(stage, layer, j, sem):
        order = conv_orders[j]
        source, landing = ((convb, conv1), (convb1, conv2), (convb2, conv3))[stage]
        dims = base
        for one in order[:stage]:
            dims = without(dims, one)
        scatter(source, landing, (layer, j), dims, order[stage], sem)

    def conv_take(stage, layer, j, sem):
        order = conv_orders[j]
        source, landing = ((convb, conv1), (convb1, conv2), (convb2, conv3))[stage]
        dims = base
        for one in order[:stage]:
            dims = without(dims, one)
        total = gather(source, landing, (layer, j), dims, order[stage], sem)
        if stage == 0:
            convb1[layer, j] = total.astype(BF)
        elif stage == 1:
            convb2[layer, j] = total.astype(BF)
        else:
            gconv_out[layer, :, j * LANE : (j + 1) * LANE] = total

    for j in range(4):
        conv_core(1, j, j)
        conv_send(0, 1, j, 16 + j)

    def first_body(i, sums):
        start = pl.multiple_of(i * 32, 32)
        out, sums = norm_back(gh[pl.ds(start, 32), :], gain0, xhat0, der0, rstd0, start, None, 32, sums)
        gf[pl.ds(start, 32), :] = out.astype(BF)
        return sums

    sums0 = lax.fori_loop(0, 16, first_body, zeros)
    put_norm(0, sums0)

    grad_first = gf[...]
    for h in range(8):
        part = dot(act[:, h * 128 : (h + 1) * 128], grad_first, TN).astype(BF)
        for j in range(4):
            convp[0, j, h // 2, (h % 2) * 2 : (h % 2) * 2 + 2] = part[:, j * LANE : (j + 1) * LANE].reshape(2, 2, 4, 8, LANE)
    for j in range(4):
        launch(remote(convp.at[0, j, :, :, 1 - c], convr.at[0, j], rs_s.at[8 + j, 3], rs_r.at[8 + j], mate))
    to_mate = remote(nrm, nrmr, nm_s.at[0, 0], nm_r.at[0], mate)
    to_mate.start()

    for m in range(4):
        await_bytes(projr.at[m], rs_r.at[4 + m])
        projb[m] = (projp[m, :, :, c].astype(F32) + projr[m].astype(F32)).astype(BF)
        scatter(projb, proj1, (m,), ("z", "x"), proj_orders[m][0], 12 + m)
    for j in range(4):
        conv_core(0, j, 8 + j)
        conv_send(0, 0, j, 20 + j)
    for j in range(4):
        conv_take(0, 1, j, 16 + j)
        conv_send(1, 1, j, 24 + j)
    for m in range(4):
        projb1[m] = gather(projb, proj1, (m,), ("z", "x"), proj_orders[m][0], 12 + m).astype(BF)
        scatter(projb1, proj2, (m,), (proj_orders[m][1],), proj_orders[m][1], 36 + m)

    for h in range(2):
        gx[pl.ds(h * 256, 256), :] = dot(gf[pl.ds(h * 256, 256), :], wv[0], NT)

    @pl.loop(0, 8)
    def _(i):
        for h in range(2):
            rows = gx[pl.ds(pl.multiple_of(h * 256 + i * 32, 32), 32), :]
            for k in range(2):
                for j in range(4):
                    xo[j, pl.ds(2 * h + k, 32, stride=4), :] = rows[:, k * 512 + j * LANE : k * 512 + (j + 1) * LANE]
        out = jnp.concatenate([xo[j] for j in range(4)], axis=1)
        gfv[pl.ds(pl.multiple_of(i * 128, 128), 128), :] = out.astype(BF)

    feat_out = pltpu.make_async_copy(gfv, gfeat_out, out_sem.at[0])
    feat_out.start()

    turn = ((iota((128, 1024), 1) >> 3) == iota((128, 1024), 0)).astype(F32).astype(BF)
    pick_t = (iota((512, 128), 1) == dp).astype(F32).astype(BF)
    wanted_t = dot(dot(pick_t, table, NT).astype(BF), turn)
    r_id = (iota((512, 1024), 1) & 7).astype(F32)
    c_id = iota((512, 1024), 0).astype(F32)
    query[...] = (wanted_t * 8.0 + r_id == c_id).astype(F32).astype(BF)
    await_bytes(precv, a2a_r.at[1])
    packv[...] = dot(query[...], precv[...].reshape(1024, 320)).astype(BF)
    pack_out = pltpu.make_async_copy(packv, packed_out, out_sem.at[1])
    pack_out.start()

    def norm_stage(stage, axis):
        copies = []
        for k in range(1, 4):
            copies.append(
                remote(nrm, nrm1.at[stage, k - 1], nm_s.at[1 + stage, k - 1], nm_r.at[1 + stage], peer(axis, k))
            )
            copies[-1].start()
        return copies

    def norm_take(stage, copies):
        await_bytes(nrm1.at[stage], nm_r.at[1 + stage])
        for one in copies:
            one.wait_send()
        nrm[...] = nrm[...] + nrm1[stage, 0] + nrm1[stage, 1] + nrm1[stage, 2]

    await_bytes(nrmr, nm_r.at[0])
    to_mate.wait_send()
    nrm[...] = nrm[...] + nrmr[...]
    moving = norm_stage(0, "x")
    norm_take(0, moving)
    for j in range(4):
        conv_take(0, 0, j, 20 + j)
        conv_send(1, 0, j, 28 + j)
    moving = norm_stage(1, "y")
    norm_take(1, moving)
    for j in range(4):
        conv_take(1, 1, j, 24 + j)
        conv_send(2, 1, j, 32 + j)
    for m in range(4):
        projb2[m] = gather(projb1, proj2, (m,), (proj_orders[m][1],), proj_orders[m][1], 36 + m).astype(BF)
    scatter(projb2, proj3, (), ("y",), "y", 40)
    for j in range(4):
        conv_take(1, 0, j, 28 + j)
        conv_send(2, 0, j, 44 + j)
    moving = norm_stage(2, "z")
    norm_take(2, moving)
    gnorm_out[...] = nrm[...]
    for j in range(4):
        conv_take(2, 1, j, 32 + j)
    gproj_out[...] = gather(projb2, proj3, (), ("y",), "y", 40)
    for j in range(4):
        conv_take(2, 0, j, 44 + j)

    for one in sends:
        one.wait_send()
    await_bytes(gsend.at[pl.ds(0, 127)], a2a_s.at[0])
    await_bytes(precv.at[pl.ds(0, 127)], a2a_s.at[1])
    feat_out.wait()
    pack_out.wait()


def local(features, lengths, dests, offsets, conv_weight, norm_gain, norm_shift, proj_weight, grad_packed):
    steps = jnp.arange(8, dtype=jnp.int32)[None, :]
    rows = dests[:, None] * 8 + (offsets & 7)[:, None] + steps
    target = jnp.where(steps < lengths[:, None], rows, -1).reshape(1, 256)
    pair_dest, pair_block = dests[0::2], offsets[0::2] >> 3
    named = pair_dest[:, None] == jnp.arange(LANE, dtype=jnp.int32)[None, :]
    index_row = jnp.min(jnp.where(named, pair_block[:, None], 64), axis=0, keepdims=True).astype(F32)
    vmem = pl.BlockSpec(memory_space=pltpu.VMEM)
    hbm = pl.BlockSpec(memory_space=pl.ANY)
    V = pltpu.VMEM
    D = pltpu.SemaphoreType.DMA
    scratch = [
        V((1024, 512), BF), V((2, 1024, 512), BF), V((512, 320), BF), V((4, 128, LANE), F32),
        V((512, 1024), BF), V((512, 512), F32), V((512, 512), F32), V((512, 512), F32), V((512, LANE), F32),
        V((256, 512), F32), V((256, 512), F32), V((256, LANE), F32),
        V((256, 1024), BF), V((256, 512), BF), V((256, 512), BF),
        V((4, 8, 4, 1, LANE), F32), V((512, 1024), BF), V((128, 8, 320), BF), V((4, 32, 8, 320), BF),
        V((4, 32, 8, 320), BF), V((128, 8, 320), BF), V((4, 2, 256, 320), BF), V((512, 320), BF),
        V((512, 512), F32), V((512, 512), BF), V((512, 1024), F32), V((4, 128, LANE), F32), V((1024, 512), BF),
        V((2, 4, 4, 4, 2, 4, 8, LANE), BF), V((2, 4, 4, 4, 4, 8, LANE), BF), V((2, 4, 4, 4, 4, 8, LANE), BF),
        V((2, 4, 3, 4, 4, 8, LANE), BF), V((2, 4, 4, 4, 8, LANE), BF),
        V((2, 4, 3, 4, 8, LANE), BF), V((2, 4, 4, 8, LANE), BF), V((2, 4, 3, 8, LANE), BF),
        V((4, 4, 4, 2, 16, 320), BF), V((4, 4, 4, 16, 320), BF), V((4, 4, 4, 16, 320), BF),
        V((4, 3, 4, 16, 320), BF), V((4, 4, 16, 320), BF), V((4, 3, 16, 320), BF), V((4, 16, 320), BF), V((3, 16, 320), BF),
        V((16, LANE), F32), V((16, LANE), F32), V((3, 3, 16, LANE), F32),
        D((4,)), D((2,)), D((13,)), D((3,)), D((7,)), D((7,)), D((2,)), D((2,)), D((48, 4)), D((48,)), D((4, 3)), D((4,)),
    ]
    packed, gfeat, gconv, gproj, gnorm = pl.pallas_call(
        kernel,
        out_shape=(
            jax.ShapeDtypeStruct((512, 320), BF),
            jax.ShapeDtypeStruct((1024, 512), BF),
            jax.ShapeDtypeStruct((2, 8, 512), F32),
            jax.ShapeDtypeStruct((16, 320), F32),
            jax.ShapeDtypeStruct((16, LANE), F32),
        ),
        in_specs=[vmem] * 4 + [hbm] * 4,
        out_specs=(hbm, hbm, vmem, vmem, vmem),
        scratch_shapes=scratch,
        compiler_params=pltpu.CompilerParams(collective_id=0, has_side_effects=True),
    )(
        index_row, target, norm_gain, norm_shift, features.reshape(1024, 512), conv_weight,
        proj_weight.reshape(2, 256, 320), grad_packed,
    )
    at = (lax.axis_index("dp") * 4 + lax.axis_index("mp")) * 8
    grad_norm = lax.dynamic_slice(gnorm.reshape(2, 1024), (0, at), (2, 8))
    return packed, gfeat.reshape(32, 32, 512), gconv, grad_norm, gproj


def solution(mesh):
    return jax.shard_map(
        local,
        mesh=mesh,
        in_specs=(
            P(("dp", "mp"), None, None),
            P(("dp", "mp")),
            P(("dp", "mp")),
            P(("dp", "mp")),
            P(),
            P(),
            P(),
            P(None, "mp"),
            P("dp", "mp"),
        ),
        out_specs=(
            P("dp", "mp"),
            P(("dp", "mp"), None, None),
            P(None, ("dp", "mp"), None),
            P(None, ("dp", "mp")),
            P("dp", "mp"),
        ),
        check_vma=False,
    )
```

time: 303 us -> 85.4 us (0.28)
  the two profiles are of different devices: /device:TPU:1 before, /device:TPU:0 now
where the time goes in v1:
time: 85.4 us; the launch traced here: 85.1 us
  Pallas kernels  69.7 us (82%)
  local copies, waits for them, and re-layouts  12.7 us (15%)
  other arithmetic  2.02 us (2%)
    pallas_call x1, Pallas kernels, local(): pl.pallas_call(kernel, out_shape=(jax.ShapeDtypeStruct((512, 320), BF), j...  69.7 us
    unnamed x10, local copies, waits for them, and re-layouts  9.22 us

profile of v1, /device:TPU:0, one launch (start us, length us, event | category | flops | bytes accessed | tf_op | source)
XLA Modules:
  0.0 85.1 jit_solution(18444509327202740422)
XLA Ops:
  0.6 0.8 slice.7
  1.4 0.8 slice.6
  2.1 0.1 select_reduce_fusion
  2.2 0.5 convert_bitcast_fusion.idx_ref
  2.8 0.7 and_add_fusion
  3.4 0.7 add_select_fusion
  4.2 0.7 select_n.23.tgt_ref
  4.8 1.9 %copy.20 = bf16[512,320]{1,0:T(8,128)(2,1)} copy(bf16[512,320]{0,1:T(8,128)(2,1)} %param.16) | data formatting | bytes 655360 | tf_op args[7]
  6.7 1.9 %copy.21.gp_hbm = bf16[512,320]{1,0:T(8,128)(2,1)} copy(bf16[512,320]{0,1:T(8,128)(2,1)} %param.17) | data formatting | bytes 655360 | tf_op args[8]
  8.6 69.7 %shard_map.128 = (bf16[512,320]{1,0:T(8,128)(2,1)}, bf16[1024,512]{1,0:T(8,128)(2,1)}, f32[2,8,512]{2,1,0:T(8,128)}, f32[16,320]{1,0:T(8,128)}, f32[16,128]{1,0:T(8,128)}) custom-call(f32[1,128]{1,0:T(1,128)} %convert_bitcast_fusion.idx_ref, s32[1,256]{1,0:T(1,128)} %select_n.23.tgt_ref, f32[2,512]{1,0:T(2,128)} %gain_ref.1, f32[2,512]{1,0:T(2,128)} %shift_ref.1, ...), custom_call_target="tpu_custom_call" | custom-call | tf_op jit(solution)/shard_map/pallas_call | solution.py:455
  78.3 0.0 copy-start
  78.3 0.0 copy-start.1
  78.3 1.9 %copy.22 = bf16[512,320]{0,1:T(8,128)(2,1)} copy(bf16[512,320]{1,0:T(8,128)(2,1)} %get-tuple-element.25) | data formatting | bytes 655360
  80.2 0.7 reshape.90
  80.9 0.6 constant_dynamic-slice_fusion
  81.5 2.3 %copy.26 = bf16[32,32,512]{2,1,0:T(8,128)(2,1)} copy(bf16[32,32,512]{2,1,0:T(8,128)(2,1)} %bitcast.7) | data formatting | bytes 2097152
  83.8 0.0 copy-done
  83.8 0.6 copy.27
  84.4 0.0 copy-done.1
  84.4 0.6 copy.28
  (1 shorter events, 0.0 us)
Async XLA Ops:
  78.3 5.6 %copy-start = (f32[2,8,512]{2,1,0:T(8,128)S(1)}, f32[2,8,512]{2,1,0:T(8,128)}, u32[]{:S(2)}) copy-start(f32[2,8,512]{2,1,0:T(8,128)} %get-tuple-element.37) | copy-start | bytes 98308
  78.3 6.2 %copy-start.1 = (f32[16,320]{1,0:T(8,128)S(1)}, f32[16,320]{1,0:T(8,128)}, u32[]{:S(2)}) copy-start(f32[16,320]{1,0:T(8,128)} %get-tuple-element.39) | copy-start | bytes 61444

commit v2 on v1

v2 whole, which is shorter than its diff:
```python
import jax
import jax.numpy as jnp
from jax import lax
from jax.experimental import pallas as pl
from jax.experimental.pallas import tpu as pltpu
from jax.sharding import PartitionSpec as P

EPSILON = 1e-05
BF = jnp.bfloat16
F32 = jnp.float32
MESH = pl.DeviceIdType.MESH
NN = (((1,), (0,)), ((), ()))
NT = (((1,), (1,)), ((), ()))
TN = (((0,), (0,)), ((), ()))
LANE = 128


def dot(a, b, dims=NN):
    return lax.dot_general(a, b, dims, preferred_element_type=F32)


def iota(shape, dim):
    return lax.broadcasted_iota(jnp.int32, shape, dim)


def kernel(
    len_ref, dest_ref, off_ref, gain_ref, shift_ref, feat_hbm, weight_hbm, proj_hbm, gp_hbm,
    packed_out, gfeat_out, gconv_out, gproj_out, gnorm_out,
    xb, wv, gpv, xf, act, pre, xhat0, der0, rstd0, xhat1, der1, rstd1, hid, frm, slots,
    tbl, query, gsend, grecv, psend, precv, pall,
    gh, gf, gx, xo,
    convp, convr, convb, conv1, convb1, conv2, convb2, conv3,
    projp, projr, projb, proj1, projb1, proj2, projb2, proj3,
    nrm, nrmr, nrm1,
    in_sem, idx_s, idx_r, ag_s, ag_r, a2a_s, a2a_r, rs_s, rs_r, nm_s, nm_r,
):
    dp = lax.axis_index("dp")
    y = lax.axis_index("mp")
    z, q = dp // 8, dp % 8
    x, c = q // 2, q % 2
    d = dp * 4 + y

    def dp_of(zz, xx, cc):
        return zz * 8 + xx * 2 + cc

    def remote(src, dst, ssem, rsem, to):
        return pltpu.make_async_remote_copy(
            src_ref=src, dst_ref=dst, send_sem=ssem, recv_sem=rsem, device_id=to, device_id_type=MESH
        )

    def await_bytes(ref, sem):
        pltpu.make_async_copy(ref, ref, sem).wait()

    loads = [
        pltpu.make_async_copy(feat_hbm, xb, in_sem.at[0]),
        pltpu.make_async_copy(weight_hbm, wv, in_sem.at[1]),
        pltpu.make_async_copy(proj_hbm, pall.at[y], in_sem.at[2]),
        pltpu.make_async_copy(gp_hbm, gpv, in_sem.at[3]),
    ]
    for one in (2, 0, 1, 3):
        loads[one].start()

    partners = (
        [(dp, (y + k) % 4) for k in range(1, 4)]
        + [(z * 8 + (q + k) % 8, y) for k in range(1, 8)]
        + [(((z + k) % 4) * 8 + q, y) for k in range(1, 4)]
    )
    barrier = pltpu.get_barrier_semaphore()
    for to in partners:
        pl.semaphore_signal(barrier, inc=1, device_id=to, device_id_type=MESH)

    lane = iota((1, LANE), 1)
    row = jnp.full((1, LANE), 64, jnp.int32)
    for p in range(16):
        row = jnp.where(lane == dest_ref[2 * p], off_ref[2 * p] >> 3, row)
    tbl[z, q, y] = row.astype(F32)
    lane = iota((1, 256), 1)
    utterance, step = lane >> 3, lane & 7
    target = jnp.full((1, 256), -1, jnp.int32)
    for u in range(32):
        at = jnp.where(step < len_ref[u], dest_ref[u] * 8 + (off_ref[u] & 7) + step, -1)
        target = jnp.where(utterance == u, at, target)
    place = (iota((256, 256), 0) == target).astype(F32).astype(BF)

    loads[0].wait()

    @pl.loop(0, 8)
    def _(i):
        rows = xb[pl.ds(pl.multiple_of(i * 128, 128), 128), :].astype(F32)
        for j in range(4):
            xf[j] = rows[:, j * LANE : (j + 1) * LANE]
        for k in range(4):
            part = jnp.concatenate([xf[j, pl.ds(k, 32, stride=4), :] for j in range(4)], axis=1)
            act[pl.ds(pl.multiple_of((k // 2) * 256 + i * 32, 32), 32), (k % 2) * 512 : (k % 2) * 512 + 512] = part.astype(BF)

    pl.semaphore_wait(barrier, len(partners))

    sends = []

    def launch(copy):
        copy.start()
        sends.append(copy)

    for k in range(1, 4):
        launch(remote(tbl.at[z, q, y], tbl.at[z, q, y], idx_s.at[k - 1], idx_r.at[0], (dp, (y + k) % 4)))
    loads[2].wait()
    up, down, far = (y + 1) % 4, (y + 3) % 4, (y + 2) % 4
    launch(remote(pall.at[y, c], pall.at[y, c], ag_s.at[0], ag_r.at[0], (dp, up)))
    launch(remote(pall.at[y, c], pall.at[y, c], ag_s.at[1], ag_r.at[1], (dp, down)))

    loads[1].wait()
    pre[...] = dot(act[...], wv[0])

    await_bytes(tbl.at[z, q, pl.ds(0, 3)], idx_r.at[0])
    for k in range(1, 8):
        launch(remote(tbl.at[z, q], tbl.at[z, q], idx_s.at[2 + k], idx_r.at[1], (z * 8 + (q + k) % 8, y)))

    def norm_gelu(source, gain, shift, xhat, der, rstd, start, count):
        v = source[pl.ds(start, count), :]
        mean = jnp.mean(v, axis=-1, keepdims=True)
        centred = v - mean
        spread = jnp.mean(centred * centred, axis=-1, keepdims=True)
        inv = lax.rsqrt(spread + EPSILON)
        normal = centred * inv
        arg = normal * gain + shift
        cdf = 0.5 + 0.5 * lax.erf(arg * (2.0**-0.5))
        xhat[pl.ds(start, count), :] = normal
        der[pl.ds(start, count), :] = cdf + arg * (jnp.exp(-0.5 * arg * arg) * 0.3989422804014327)
        rstd[pl.ds(start, count), :] = jnp.broadcast_to(inv, (count, LANE))
        return arg * cdf

    gain0, shift0 = gain_ref[0:1, :], shift_ref[0:1, :]
    gain1, shift1 = gain_ref[1:2, :], shift_ref[1:2, :]

    def first_rows(lo, hi):
        @pl.loop(lo, hi)
        def _(i):
            start = pl.multiple_of(i * 32, 32)
            for h in range(2):
                out = norm_gelu(pre, gain0, shift0, xhat0, der0, rstd0, pl.multiple_of(start + h * 256, 32), 32)
                hid[pl.ds(start, 32), h * 512 : (h + 1) * 512] = out.astype(BF)

    first_rows(0, 4)

    await_bytes(tbl.at[z, pl.ds(0, 7)], idx_r.at[1])
    for k in range(1, 4):
        launch(remote(tbl.at[z], tbl.at[z], idx_s.at[9 + k], idx_r.at[2], (((z + k) % 4) * 8 + q, y)))

    first_rows(4, 8)
    await_bytes(pall.at[down, c], ag_r.at[0])
    launch(remote(pall.at[down, c, pl.ds(0, 80)], pall.at[down, c, pl.ds(0, 80)], ag_s.at[2], ag_r.at[2], (dp, up)))
    await_bytes(pall.at[up, c], ag_r.at[1])
    launch(remote(pall.at[up, c, pl.ds(80, 80)], pall.at[up, c, pl.ds(80, 80)], ag_s.at[3], ag_r.at[3], (dp, down)))

    loads[3].wait()
    await_bytes(tbl.at[pl.ds(0, 3)], idx_r.at[2])
    table = tbl[...].reshape(128, LANE).astype(BF)
    pick = (iota((128, 512), 0) == dp).astype(F32).astype(BF)
    blocks = dot(table, pick).astype(BF)
    row_id = iota((256, 512), 0)
    column = (iota((256, 512), 1) - (row_id & 7)).astype(F32)

    own_g = pltpu.make_async_copy(gsend.at[d], grecv.at[y, dp], a2a_r.at[0])
    for turn in range(4):
        part = (z + turn) % 4
        spread = ((iota((256, 128), 0) >> 3) + part * 32 == iota((256, 128), 1)).astype(F32).astype(BF)
        one_hot = (dot(spread, blocks) * 8.0 == column).astype(F32).astype(BF)
        query[pl.ds(pl.multiple_of(part * 256, 256), 256), :] = one_hot
        gsend[pl.ds(part * 32, 32)] = dot(one_hot, gpv[...], NT).astype(BF).reshape(32, 8, 320)
        if turn == 0:
            own_g.start()

        @pl.loop(0, 8)
        def _(k):
            to = part * 8 + (q + k) % 8
            for m in range(4):
                if turn == 0 and m == 0:

                    @pl.when(k > 0)
                    def _():
                        remote(gsend.at[to * 4 + y], grecv.at[y, dp], a2a_s.at[0], a2a_r.at[0], (to, y)).start()
                else:
                    side = (y + m) % 4
                    remote(gsend.at[to * 4 + side], grecv.at[y, dp], a2a_s.at[0], a2a_r.at[0], (to, side)).start()

    await_bytes(pall.at[far, c, pl.ds(0, 80)], ag_r.at[2])
    await_bytes(pall.at[far, c, pl.ds(80, 80)], ag_r.at[3])
    mate = (dp_of(z, x, 1 - c), y)
    for n, at in enumerate((up, down, far)):
        launch(remote(pall.at[at, c], pall.at[at, c], ag_s.at[4 + n], ag_r.at[4 + n], mate))

    pre[pl.ds(0, 256), :] = dot(hid[...], wv[1])

    @pl.loop(0, 4)
    def _(i):
        for h in range(2):
            start = pl.multiple_of(i * 64 + h * 32, 32)
            out = norm_gelu(pre, gain1, shift1, xhat1, der1, rstd1, start, 32)
            frm[pl.ds(start, 32), :] = out.astype(BF)

    slots[...] = dot(place, frm[...]).astype(BF)
    for n, at in enumerate((up, down, far)):
        await_bytes(pall.at[at, 1 - c], ag_r.at[4 + n])
    for m in range(4):
        psend[m] = dot(slots[...], pall[m].reshape(320, 512), NT).astype(BF).reshape(32, 8, 320)

    own_p = pltpu.make_async_copy(psend.at[y, dp], precv.at[d], a2a_r.at[1])
    own_p.start()

    @pl.loop(0, 32)
    def _(k):
        to = (dp + k) % 32
        for m in range(4):
            side = (y + m) % 4
            copy = remote(psend.at[side, to], precv.at[d], a2a_s.at[1], a2a_r.at[1], (to, side))
            if m == 0:
                pl.when(k > 0)(copy.start)
            else:
                copy.start()

    await_bytes(grecv, a2a_r.at[0])

    total = None
    for m in range(4):
        part = dot(grecv[m].reshape(256, 320), pall[m].reshape(320, 512))
        total = part if total is None else total + part
    grad_frames = dot(place, total.astype(BF), TN)
    gh[pl.ds(0, 256), :] = grad_frames

    sizes = dict(x=x, y=y, z=z)

    def peer(axis, k):
        if axis == "x":
            return (dp_of(z, (x + k) % 4, c), y)
        if axis == "z":
            return (dp_of((z + k) % 4, x, c), y)
        return (dp, (y + k) % 4)

    def chunk(ref, lead, dims, axis, at):
        pos = dims.index(axis)
        return ref.at[tuple(lead) + (slice(None),) * pos + (at,)]

    def scatter(source, landing, lead, dims, axis, sem):
        for k in range(1, 4):
            at = (sizes[axis] + k) % 4
            launch(
                remote(
                    chunk(source, lead, dims, axis, at),
                    landing.at[tuple(lead) + (k - 1,)],
                    rs_s.at[sem, k - 1],
                    rs_r.at[sem],
                    peer(axis, k),
                )
            )

    def gather(source, landing, lead, dims, axis, sem):
        await_bytes(landing.at[tuple(lead) + (pl.ds(0, 3),)], rs_r.at[sem])
        total = chunk(source, lead, dims, axis, sizes[axis])[...].astype(F32)
        for k in range(3):
            total = total + landing[tuple(lead) + (k,)].astype(F32)
        return total

    def norm_back(upstream, gain, xhat, der, rstd, start, count, sums):
        dy = upstream * der[pl.ds(start, count), :]
        normal = xhat[pl.ds(start, count), :]
        dyn = dy * normal
        dg = sums[0] + dyn.reshape(count // 8, 8, 512).sum(axis=0)
        ds = sums[1] + dy.reshape(count // 8, 8, 512).sum(axis=0)
        mean_d = jnp.mean(dy * gain, axis=-1, keepdims=True)
        mean_dn = jnp.mean(dyn * gain, axis=-1, keepdims=True)
        inv = rstd[pl.ds(start, count), :][:, 0:1]
        return inv * (dy * gain - mean_d - normal * mean_dn), (dg, ds)

    def put_norm(layer, sums):
        for half in range(2):
            row = sums[half].sum(axis=0, keepdims=True)
            for j in range(4):
                nrm[layer * 8 + half * 4 + j : layer * 8 + half * 4 + j + 1, :] = row[:, j * LANE : (j + 1) * LANE]

    zeros = (jnp.zeros((8, 512), F32), jnp.zeros((8, 512), F32))

    def second_body(i, sums):
        for h in range(2):
            start = pl.multiple_of(i * 64 + h * 32, 32)
            out, sums = norm_back(gh[pl.ds(start, 32), :], gain1, xhat1, der1, rstd1, start, 32, sums)
            gf[pl.ds(start, 32), :] = out.astype(BF)
        return sums

    sums1 = lax.fori_loop(0, 4, second_body, zeros)
    put_norm(1, sums1)
    grad_second = gf[pl.ds(0, 256), :]
    for h in range(2):
        gh[pl.ds(h * 256, 256), :] = dot(grad_second, wv[1, pl.ds(h * 512, 512), :], NT).astype(BF).astype(F32)

    for h in range(8):
        part = dot(hid[:, h * 128 : (h + 1) * 128], grad_second, TN).astype(BF)
        for j in range(4):
            convp[1, j, h // 2, (h % 2) * 2 : (h % 2) * 2 + 2] = part[:, j * LANE : (j + 1) * LANE].reshape(2, 2, 4, 8, LANE)
    for j in range(4):
        launch(remote(convp.at[1, j, :, :, 1 - c], convr.at[1, j], rs_s.at[j, 3], rs_r.at[j], mate))

    for m in range(4):
        part = dot(slots[...], grecv[m].reshape(256, 320), TN).astype(BF)
        projp[m] = part.reshape(4, 4, 2, 16, 320)
    for m in range(4):
        launch(remote(projp.at[m, :, :, 1 - c], projr.at[m], rs_s.at[4 + m, 3], rs_r.at[4 + m], mate))

    conv_orders = (
        (("x", "y", "z"), ("y", "z", "x"), ("z", "x", "y"), ("x", "z", "y")),
        (("y", "x", "z"), ("y", "z", "x"), ("y", "x", "z"), ("y", "z", "x")),
    )
    proj_orders = (("x", "z"), ("z", "x"), ("x", "z"), ("z", "x"))

    def conv_core(layer, j, sem):
        await_bytes(convr.at[layer, j], rs_r.at[sem])
        convb[layer, j] = (
            convp[layer, j, :, :, c].astype(F32) + convr[layer, j].astype(F32)
        ).astype(BF)

    def without(dims, axis):
        return tuple(one for one in dims if one != axis)

    base = ("z", "x", "y")

    def conv_send(stage, layer, j, sem):
        order = conv_orders[layer][j]
        source, landing = ((convb, conv1), (convb1, conv2), (convb2, conv3))[stage]
        dims = base
        for one in order[:stage]:
            dims = without(dims, one)
        scatter(source, landing, (layer, j), dims, order[stage], sem)

    def conv_take(stage, layer, j, sem):
        order = conv_orders[layer][j]
        source, landing = ((convb, conv1), (convb1, conv2), (convb2, conv3))[stage]
        dims = base
        for one in order[:stage]:
            dims = without(dims, one)
        total = gather(source, landing, (layer, j), dims, order[stage], sem)
        if stage == 0:
            convb1[layer, j] = total.astype(BF)
        elif stage == 1:
            convb2[layer, j] = total.astype(BF)
        else:
            gconv_out[layer, :, j * LANE : (j + 1) * LANE] = total

    for j in range(4):
        conv_core(1, j, j)
        conv_send(0, 1, j, 16 + j)

    def first_body(i, sums):
        for h in range(2):
            start = pl.multiple_of(i * 64 + h * 32, 32)
            out, sums = norm_back(gh[pl.ds(start, 32), :], gain0, xhat0, der0, rstd0, start, 32, sums)
            gf[pl.ds(start, 32), :] = out.astype(BF)
        return sums

    sums0 = lax.fori_loop(0, 8, first_body, zeros)
    put_norm(0, sums0)
    to_mate = remote(nrm, nrmr, nm_s.at[0, 0], nm_r.at[0], mate)
    to_mate.start()

    grad_first = gf[...]
    for h in range(8):
        part = dot(act[:, h * 128 : (h + 1) * 128], grad_first, TN).astype(BF)
        for j in range(4):
            convp[0, j, h // 2, (h % 2) * 2 : (h % 2) * 2 + 2] = part[:, j * LANE : (j + 1) * LANE].reshape(2, 2, 4, 8, LANE)
    for j in range(4):
        launch(remote(convp.at[0, j, :, :, 1 - c], convr.at[0, j], rs_s.at[8 + j, 3], rs_r.at[8 + j], mate))

    def norm_stage(stage, axis):
        copies = []
        for k in range(1, 4):
            copies.append(
                remote(nrm, nrm1.at[stage, k - 1], nm_s.at[1 + stage, k - 1], nm_r.at[1 + stage], peer(axis, k))
            )
            copies[-1].start()
        return copies

    def norm_take(stage, copies):
        await_bytes(nrm1.at[stage], nm_r.at[1 + stage])
        for one in copies:
            one.wait_send()
        nrm[...] = nrm[...] + nrm1[stage, 0] + nrm1[stage, 1] + nrm1[stage, 2]

    await_bytes(nrmr, nm_r.at[0])
    to_mate.wait_send()
    nrm[...] = nrm[...] + nrmr[...]
    moving = norm_stage(0, "x")

    for m in range(4):
        await_bytes(projr.at[m], rs_r.at[4 + m])
        projb[m] = (projp[m, :, :, c].astype(F32) + projr[m].astype(F32)).astype(BF)
        scatter(projb, proj1, (m,), ("z", "x"), proj_orders[m][0], 12 + m)
    for j in range(4):
        conv_core(0, j, 8 + j)
        conv_send(0, 0, j, 20 + j)

    for h in range(2):
        gx[pl.ds(h * 256, 256), :] = dot(gf[pl.ds(h * 256, 256), :], wv[0], NT)

    norm_take(0, moving)
    moving = norm_stage(1, "y")

    for j in range(4):
        conv_take(0, 1, j, 16 + j)
        conv_send(1, 1, j, 24 + j)

    @pl.loop(0, 8)
    def _(i):
        for h in range(2):
            rows = gx[pl.ds(pl.multiple_of(h * 256 + i * 32, 32), 32), :]
            for k in range(2):
                for j in range(4):
                    xo[j, pl.ds(2 * h + k, 32, stride=4), :] = rows[:, k * 512 + j * LANE : k * 512 + (j + 1) * LANE]
        out = jnp.concatenate([xo[j] for j in range(4)], axis=1)
        gfeat_out[pl.ds(pl.multiple_of(i * 128, 128), 128), :] = out.astype(BF)

    for m in range(4):
        projb1[m] = gather(projb, proj1, (m,), ("z", "x"), proj_orders[m][0], 12 + m).astype(BF)
        scatter(projb1, proj2, (m,), (proj_orders[m][1],), proj_orders[m][1], 36 + m)

    norm_take(1, moving)
    moving = norm_stage(2, "z")
    for j in range(4):
        conv_take(0, 0, j, 20 + j)
        conv_send(1, 0, j, 28 + j)

    await_bytes(precv, a2a_r.at[1])
    packed_out[...] = dot(precv[...].reshape(1024, 320), query[...], TN).astype(BF)

    for j in range(4):
        conv_take(1, 1, j, 24 + j)
        conv_send(2, 1, j, 32 + j)
    for m in range(4):
        projb2[m] = gather(projb1, proj2, (m,), (proj_orders[m][1],), proj_orders[m][1], 36 + m).astype(BF)
    scatter(projb2, proj3, (), ("y",), "y", 40)
    for j in range(4):
        conv_take(1, 0, j, 28 + j)
        conv_send(2, 0, j, 44 + j)
    norm_take(2, moving)
    gnorm_out[...] = nrm[...]
    for j in range(4):
        conv_take(2, 1, j, 32 + j)
    gproj_out[...] = gather(projb2, proj3, (), ("y",), "y", 40)
    for j in range(4):
        conv_take(2, 0, j, 44 + j)

    for one in sends:
        one.wait_send()
    await_bytes(gsend.at[pl.ds(0, 127)], a2a_s.at[0])
    await_bytes(precv.at[pl.ds(0, 127)], a2a_s.at[1])


def finish(
    packed_in, gfeat_in, gconv_in, gproj_in, gnorm_in, packed_out, gfeat_out, gconv_out, gproj_out, gnorm_out, sem
):
    copies = [
        pltpu.make_async_copy(packed_in, packed_out, sem.at[0]),
        pltpu.make_async_copy(gfeat_in, gfeat_out, sem.at[1]),
        pltpu.make_async_copy(gconv_in, gconv_out, sem.at[2]),
        pltpu.make_async_copy(gproj_in, gproj_out, sem.at[3]),
    ]
    for one in (1, 0, 2, 3):
        copies[one].start()
    d = lax.axis_index("dp") * 4 + lax.axis_index("mp")
    for layer in range(2):
        row = gnorm_in[pl.ds(layer * 8 + d // 16, 1), :]
        turned = pltpu.roll(row, LANE - (d % 16) * 8, 1)
        gnorm_out[layer : layer + 1, :] = turned[:, 0:8]
    for one in copies:
        one.wait()


def local(features, lengths, dests, offsets, conv_weight, norm_gain, norm_shift, proj_weight, grad_packed):
    vmem = pl.BlockSpec(memory_space=pltpu.VMEM)
    hbm = pl.BlockSpec(memory_space=pltpu.HBM)
    smem = pl.BlockSpec(memory_space=pltpu.SMEM)
    V = pltpu.VMEM
    D = pltpu.SemaphoreType.DMA
    scratch = [
        V((1024, 512), BF), V((2, 1024, 512), BF), V((320, 512), BF), V((4, 128, LANE), F32),
        V((512, 1024), BF), V((512, 512), F32), V((512, 512), F32), V((512, 512), F32), V((512, LANE), F32),
        V((256, 512), F32), V((256, 512), F32), V((256, LANE), F32),
        V((256, 1024), BF), V((256, 512), BF), V((256, 512), BF),
        V((4, 8, 4, 1, LANE), F32), V((1024, 512), BF), V((128, 8, 320), BF), V((4, 32, 8, 320), BF),
        V((4, 32, 8, 320), BF), V((128, 8, 320), BF), V((4, 2, 160, 512), BF),
        V((512, 512), F32), V((512, 512), BF), V((512, 1024), F32), V((4, 128, LANE), F32),
        V((2, 4, 4, 4, 2, 4, 8, LANE), BF), V((2, 4, 4, 4, 4, 8, LANE), BF), V((2, 4, 4, 4, 4, 8, LANE), BF),
        V((2, 4, 3, 4, 4, 8, LANE), BF), V((2, 4, 4, 4, 8, LANE), BF),
        V((2, 4, 3, 4, 8, LANE), BF), V((2, 4, 4, 8, LANE), BF), V((2, 4, 3, 8, LANE), BF),
        V((4, 4, 4, 2, 16, 320), BF), V((4, 4, 4, 16, 320), BF), V((4, 4, 4, 16, 320), BF),
        V((4, 3, 4, 16, 320), BF), V((4, 4, 16, 320), BF), V((4, 3, 16, 320), BF), V((4, 16, 320), BF), V((3, 16, 320), BF),
        V((16, LANE), F32), V((16, LANE), F32), V((3, 3, 16, LANE), F32),
        D((4,)), D((13,)), D((3,)), D((7,)), D((7,)), D((2,)), D((2,)), D((48, 4)), D((48,)), D((4, 3)), D((4,)),
    ]
    results = ((320, 512), BF), ((1024, 512), BF), ((2, 8, 512), F32), ((16, 320), F32), ((16, LANE), F32)
    middle = pl.pallas_call(
        kernel,
        out_shape=tuple(pltpu.VMEM(*one) for one in results),
        in_specs=[smem] * 3 + [vmem] * 2 + [hbm] * 4,
        out_specs=(vmem,) * 5,
        scratch_shapes=scratch,
        compiler_params=pltpu.CompilerParams(collective_id=0, has_side_effects=True, vmem_limit_bytes=65_400_000),
    )(
        lengths, dests, offsets, norm_gain, norm_shift, features.reshape(1024, 512), conv_weight,
        proj_weight.T.reshape(2, 160, 512), grad_packed.T,
    )
    shapes = (*results[:4], ((2, 8), F32))
    packed, gfeat, gconv, gproj, gnorm = pl.pallas_call(
        finish,
        out_shape=tuple(jax.ShapeDtypeStruct(*one) for one in shapes),
        in_specs=[vmem] * 5,
        out_specs=(hbm, hbm, hbm, hbm, vmem),
        scratch_shapes=[D((4,))],
    )(*[pltpu.with_memory_space_constraint(one, pltpu.VMEM) for one in middle])
    return packed.T, gfeat.reshape(32, 32, 512), gconv, gnorm, gproj


def solution(mesh):
    return jax.shard_map(
        local,
        mesh=mesh,
        in_specs=(
            P(("dp", "mp"), None, None),
            P(("dp", "mp")),
            P(("dp", "mp")),
            P(("dp", "mp")),
            P(),
            P(),
            P(),
            P(None, "mp"),
            P("dp", "mp"),
        ),
        out_specs=(
            P("dp", "mp"),
            P(("dp", "mp"), None, None),
            P(None, ("dp", "mp"), None),
            P(None, ("dp", "mp")),
            P("dp", "mp"),
        ),
        check_vma=False,
    )
```

time: 85.4 us -> 66.3 us (0.78)
  local copies, waits for them, and re-layouts: 12.7 us -> 0 us
  Pallas kernels: 69.7 us -> 65.5 us
  other arithmetic: 2.02 us -> 0 us
    unnamed x10 -> x0, local copies, waits for them, and re-layouts: 9.22 us -> none
    pallas_call x1 -> x2, Pallas kernels: 69.7 us -> 65.5 us  [the longest x1 63.8 us: local(): pl.pallas_call(kernel, out_shape=tuple((pltpu.VMEM(*one) for one in resul...]
    slice x2 -> x0, local copies, waits for them, and re-layouts: 1.5 us -> none  [local(): pair_dest, pair_block = (dests[0::2], offsets[0::2] >> 3)]
where the time goes in v2:
time: 66.3 us; the launch traced here: 66.2 us
  Pallas kernels  65.5 us (99%)
    pallas_call x1, Pallas kernels, local(): pl.pallas_call(kernel, out_shape=tuple((pltpu.VMEM(*one) for one in resul...  63.8 us
    pallas_call x1, Pallas kernels, local(): pl.pallas_call(finish, out_shape=tuple((jax.ShapeDtypeStruct(*one) for on...  1.69 us

profile of v2, /device:TPU:0, one launch (start us, length us, event | category | flops | bytes accessed | tf_op | source)
XLA Modules:
  0.0 66.2 jit_solution(13663815340898184895)
XLA Ops:
  0.6 63.8 %shard_map.128 = (bf16[320,512]{1,0:T(8,128)(2,1)S(1)}, bf16[1024,512]{1,0:T(8,128)(2,1)S(1)}, f32[2,8,512]{2,1,0:T(8,128)S(1)}, f32[16,320]{1,0:T(8,128)S(1)}, f32[16,128]{1,0:T(8,128)S(1)}) custom-call(s32[32]{0:T(128)} %len_ref.1, s32[32]{0:T(128)} %dest_ref.1, s32[32]{0:T(128)} %off_ref.1, f32[2,512]{1,0:T(2,128)} %gain_ref.1, f32[2,512]{1,0:T(2,128)} %shift_ref.1, ...), custom_call_target="tpu_custom_call" | custom-call | tf_op jit(solution)/shard_map/pallas_call | solution.py:498
  64.5 1.7 %shard_map.129 = (bf16[320,512]{1,0:T(8,128)(2,1)}, bf16[1024,512]{1,0:T(8,128)(2,1)}, f32[2,8,512]{2,1,0:T(8,128)}, f32[16,320]{1,0:T(8,128)}, f32[2,8]{1,0:T(2,128)}) custom-call(bf16[320,512]{1,0:T(8,128)(2,1)S(1)} %get-tuple-element.15.packed_in, bf16[1024,512]{1,0:T(8,128)(2,1)S(1)} %get-tuple-element.16.gfeat_in, ...), custom_call_target="tpu_custom_call" | custom-call | tf_op jit(solution)/shard_map/pallas_call | solution.py:510

commit v3 on v2

v3 whole, which is shorter than its diff:
```python
import jax
import jax.numpy as jnp
from jax import lax
from jax.experimental import pallas as pl
from jax.experimental.pallas import tpu as pltpu
from jax.sharding import PartitionSpec as P

EPSILON = 1e-05
BF = jnp.bfloat16
F32 = jnp.float32
MESH = pl.DeviceIdType.MESH
NN = (((1,), (0,)), ((), ()))
NT = (((1,), (1,)), ((), ()))
TN = (((0,), (0,)), ((), ()))
LANE = 128
WIDE = 384


def dot(a, b, dims=NN):
    return lax.dot_general(a, b, dims, preferred_element_type=F32)


def iota(shape, dim):
    return lax.broadcasted_iota(jnp.int32, shape, dim)


def kernel(
    len_ref, dest_ref, off_ref, gain_ref, shift_ref, feat_hbm, weight_hbm, proj_hbm, gp_hbm,
    packed_out, gfeat_out, gconv_out, gproj_out, gnorm_out,
    xb, wv, gpv, xf, act, actt, pre, xhat0, der0, rstd0, xhat1, der1, rstd1, hid, hidt, frm,
    tbl, query, gsend, grecv, fsend, frecv, pall, packin,
    gh, gf, gx, xo,
    convp, convr, convb, conv1, convb1, conv2,
    projp, projr, projb, proj1,
    nrm, nrmr, nrm1, nrm2,
    in_sem, idx_s, idx_r, ag_s, ag_r, a2a_s, a2a_r, fg_s, fg_r, rs_s, rs_r, nm_s, nm_r, pl_s, pl_r,
):
    dp = lax.axis_index("dp")
    y = lax.axis_index("mp")
    z, q = dp // 8, dp % 8
    x, c = q // 2, q % 2
    d = dp * 4 + y

    def dp_of(zz, xx, cc):
        return zz * 8 + xx * 2 + cc

    def remote(src, dst, ssem, rsem, to):
        return pltpu.make_async_remote_copy(
            src_ref=src, dst_ref=dst, send_sem=ssem, recv_sem=rsem, device_id=to, device_id_type=MESH
        )

    def await_bytes(ref, sem):
        pltpu.make_async_copy(ref, ref, sem).wait()

    loads = [
        pltpu.make_async_copy(feat_hbm, xb, in_sem.at[0]),
        pltpu.make_async_copy(weight_hbm, wv, in_sem.at[1]),
        pltpu.make_async_copy(proj_hbm, pall.at[y, pl.ds(0, 320)], in_sem.at[2]),
        pltpu.make_async_copy(gp_hbm, gpv.at[pl.ds(0, 320)], in_sem.at[3]),
    ]
    for one in (2, 0, 1, 3):
        loads[one].start()

    partners = (
        [(dp, (y + k) % 4) for k in range(1, 4)]
        + [(z * 8 + (q + k) % 8, y) for k in range(1, 8)]
        + [(((z + k) % 4) * 8 + q, y) for k in range(1, 4)]
    )
    barrier = pltpu.get_barrier_semaphore()
    for to in partners:
        pl.semaphore_signal(barrier, inc=1, device_id=to, device_id_type=MESH)

    lane = iota((1, LANE), 1)
    row = jnp.full((1, LANE), 64, jnp.int32)
    for p in range(16):
        row = jnp.where(lane == dest_ref[2 * p], off_ref[2 * p] >> 3, row)
    tbl[y, z, q] = row.astype(F32)
    lane = iota((1, 256), 1)
    utterance, step = lane >> 3, lane & 7
    target = jnp.full((1, 256), -1, jnp.int32)
    for u in range(32):
        at = jnp.where(step < len_ref[u], dest_ref[u] * 8 + (off_ref[u] & 7) + step, -1)
        target = jnp.where(utterance == u, at, target)
    place = (iota((256, 256), 0) == target).astype(F32).astype(BF)

    gpv[pl.ds(320, 64), :] = jnp.zeros((64, 512), BF)
    for m in range(4):
        pall[m, pl.ds(320, 64), :] = jnp.zeros((64, 512), BF)

    loads[0].wait()

    @pl.loop(0, 8)
    def _(i):
        rows = xb[pl.ds(pl.multiple_of(i * 128, 128), 128), :].astype(F32)
        for j in range(4):
            xf[j] = rows[:, j * LANE : (j + 1) * LANE]
        for k in range(4):
            part = jnp.concatenate([xf[j, pl.ds(k, 32, stride=4), :] for j in range(4)], axis=1)
            act[pl.ds(pl.multiple_of((k // 2) * 256 + i * 32, 32), 32), (k % 2) * 512 : (k % 2) * 512 + 512] = part.astype(BF)

    pl.semaphore_wait(barrier, len(partners))

    sends = []

    def launch(copy):
        copy.start()
        sends.append(copy)

    for k in range(1, 4):
        launch(remote(tbl.at[y, z, q], tbl.at[y, z, q], idx_s.at[k - 1], idx_r.at[0], (((z + k) % 4) * 8 + q, y)))
    loads[2].wait()
    own, others = pl.multiple_of(c * 160, 160), pl.multiple_of(160 - c * 160, 160)
    up, down, far = (y + 1) % 4, (y + 3) % 4, (y + 2) % 4
    launch(remote(pall.at[y, pl.ds(own, 160)], pall.at[y, pl.ds(own, 160)], ag_s.at[0], ag_r.at[0], (dp, up)))
    launch(remote(pall.at[y, pl.ds(own, 160)], pall.at[y, pl.ds(own, 160)], ag_s.at[1], ag_r.at[1], (dp, down)))

    loads[1].wait()
    pre[...] = dot(act[...], wv[0])

    await_bytes(tbl.at[y, pl.ds(0, 3), 0], idx_r.at[0])
    for k in range(1, 8):
        launch(remote(tbl.at[y, :, q], tbl.at[y, :, q], idx_s.at[2 + k], idx_r.at[1], (z * 8 + (q + k) % 8, y)))

    def norm_gelu(source, gain, shift, xhat, der, rstd, start, count):
        v = source[pl.ds(start, count), :]
        mean = jnp.mean(v, axis=-1, keepdims=True)
        centred = v - mean
        spread = jnp.mean(centred * centred, axis=-1, keepdims=True)
        inv = lax.rsqrt(spread + EPSILON)
        normal = centred * inv
        arg = normal * gain + shift
        cdf = 0.5 + 0.5 * lax.erf(arg * (2.0**-0.5))
        xhat[pl.ds(start, count), :] = normal
        der[pl.ds(start, count), :] = cdf + arg * (jnp.exp(-0.5 * arg * arg) * 0.3989422804014327)
        rstd[pl.ds(start, count), :] = jnp.broadcast_to(inv, (count, LANE))
        return arg * cdf

    gain0, shift0 = gain_ref[0:1, :], shift_ref[0:1, :]
    gain1, shift1 = gain_ref[1:2, :], shift_ref[1:2, :]

    def first_rows(lo, hi):
        @pl.loop(lo, hi)
        def _(i):
            start = pl.multiple_of(i * 32, 32)
            for h in range(2):
                out = norm_gelu(pre, gain0, shift0, xhat0, der0, rstd0, pl.multiple_of(start + h * 256, 32), 32)
                hid[pl.ds(start, 32), h * 512 : (h + 1) * 512] = out.astype(BF)

    first_rows(0, 8)
    pre[pl.ds(0, 256), :] = dot(hid[...], wv[1])

    @pl.loop(0, 4)
    def _(i):
        for h in range(2):
            start = pl.multiple_of(i * 64 + h * 32, 32)
            out = norm_gelu(pre, gain1, shift1, xhat1, der1, rstd1, start, 32)
            frm[pl.ds(start, 32), :] = out.astype(BF)

    fsend[...] = dot(place, frm[...]).astype(BF).reshape(32, 8, 512)

    await_bytes(tbl.at[y, :, pl.ds(0, 7)], idx_r.at[1])
    for k in range(1, 4):
        launch(remote(tbl.at[y], tbl.at[y], idx_s.at[9 + k], idx_r.at[2], (dp, (y + k) % 4)))
    own_f = pltpu.make_async_copy(fsend.at[dp], frecv.at[dp, y], a2a_r.at[1])
    own_f.start()

    @pl.loop(1, 32)
    def _(k):
        to = (dp + k) % 32
        remote(fsend.at[to], frecv.at[dp, y], a2a_s.at[1], a2a_r.at[1], (to, y)).start()

    first, last = pl.multiple_of(own, 16), pl.multiple_of(own + 80, 16)
    await_bytes(pall.at[down, pl.ds(own, 160)], ag_r.at[0])
    launch(remote(pall.at[down, pl.ds(first, 80)], pall.at[down, pl.ds(first, 80)], ag_s.at[2], ag_r.at[2], (dp, up)))
    await_bytes(pall.at[up, pl.ds(own, 160)], ag_r.at[1])
    launch(remote(pall.at[up, pl.ds(last, 80)], pall.at[up, pl.ds(last, 80)], ag_s.at[3], ag_r.at[3], (dp, down)))

    loads[3].wait()
    await_bytes(tbl.at[pl.ds(0, 3)], idx_r.at[2])
    table = jnp.concatenate([tbl[m].reshape(32, LANE) for m in range(4)], axis=0).astype(BF)
    pick = (iota((128, 512), 0) == dp).astype(F32).astype(BF)
    blocks = dot(table, pick).astype(BF)
    row_id = iota((256, 512), 0)
    column = (iota((256, 512), 1) - (row_id & 7)).astype(F32)

    own_g = pltpu.make_async_copy(gsend.at[d], grecv.at[y, dp], a2a_r.at[0])
    for turn in (2, 1, 3, 0):
        part = (z + turn) % 4
        slot = (iota((256, 128), 0) >> 3) + part * 32
        spread = ((slot & 3) * 32 + (slot >> 2) == iota((256, 128), 1)).astype(F32).astype(BF)
        one_hot = (dot(spread, blocks) * 8.0 == column).astype(F32).astype(BF)
        query[pl.ds(pl.multiple_of(part * 256, 256), 256), :] = one_hot
        gsend[pl.ds(part * 32, 32)] = dot(one_hot, gpv[...], NT).astype(BF).reshape(32, 8, WIDE)
        for along in (2, 1, 3, 0):
            for core in range(2):
                to = part * 8 + ((x + along) % 4) * 2 + (c + core) % 2
                for across in (2, 1, 3, 0):
                    side = (y + across) % 4
                    if turn or along or core or across:
                        remote(gsend.at[to * 4 + side], grecv.at[y, dp], a2a_s.at[0], a2a_r.at[0], (to, side)).start()
                    else:
                        own_g.start()

    await_bytes(pall.at[far, pl.ds(first, 80)], ag_r.at[2])
    await_bytes(pall.at[far, pl.ds(last, 80)], ag_r.at[3])
    mate = (dp_of(z, x, 1 - c), y)
    for n, at in enumerate((up, down, far)):
        launch(remote(pall.at[at, pl.ds(own, 160)], pall.at[at, pl.ds(own, 160)], ag_s.at[4 + n], ag_r.at[4 + n], mate))

    actt[...] = act[...].T
    hidt[...] = hid[...].T
    for n, at in enumerate((up, down, far)):
        await_bytes(pall.at[at, pl.ds(others, 160)], ag_r.at[4 + n])
    await_bytes(frecv.at[:, 0], a2a_r.at[1])
    await_bytes(grecv, a2a_r.at[0])
    low, high = pl.ds(0, 16), pl.ds(16, 16)
    for n, (to, half) in enumerate(((up, low), (down, high), (up, high), (down, low))):
        launch(remote(frecv.at[half, y], frecv.at[half, y], fg_s.at[n], fg_r.at[n], (dp, to)))

    total = None
    for m in range(4):
        part = dot(grecv[m].reshape(256, WIDE), pall[m])
        total = part if total is None else total + part
    grad_frames = dot(place, total.astype(BF), TN)
    gh[pl.ds(0, 256), :] = grad_frames

    sizes = dict(x=x, y=y, z=z)

    def peer(axis, k):
        if axis == "x":
            return (dp_of(z, (x + k) % 4, c), y)
        if axis == "z":
            return (dp_of((z + k) % 4, x, c), y)
        return (dp, (y + k) % 4)

    def chunk(ref, lead, dims, axis, at):
        pos = dims.index(axis)
        return ref.at[tuple(lead) + (slice(None),) * pos + (at,)]

    def scatter(source, landing, lead, dims, axis, sem):
        for k in range(1, 4):
            at = (sizes[axis] + k) % 4
            launch(
                remote(
                    chunk(source, lead, dims, axis, at),
                    landing.at[tuple(lead) + (k - 1,)],
                    rs_s.at[sem, k - 1],
                    rs_r.at[sem],
                    peer(axis, k),
                )
            )

    def gather(source, landing, lead, dims, axis, sem):
        await_bytes(landing.at[tuple(lead) + (pl.ds(0, 3),)], rs_r.at[sem])
        total = chunk(source, lead, dims, axis, sizes[axis])[...].astype(F32)
        for k in range(3):
            total = total + landing[tuple(lead) + (k,)].astype(F32)
        return total

    def norm_back(upstream, gain, xhat, der, rstd, start, count, sums):
        dy = upstream * der[pl.ds(start, count), :]
        normal = xhat[pl.ds(start, count), :]
        dyn = dy * normal
        dg = sums[0] + dyn.reshape(count // 8, 8, 512).sum(axis=0)
        ds = sums[1] + dy.reshape(count // 8, 8, 512).sum(axis=0)
        mean_d = jnp.mean(dy * gain, axis=-1, keepdims=True)
        mean_dn = jnp.mean(dyn * gain, axis=-1, keepdims=True)
        inv = rstd[pl.ds(start, count), :][:, 0:1]
        return inv * (dy * gain - mean_d - normal * mean_dn), (dg, ds)

    def put_norm(layer, sums):
        for half in range(2):
            row = sums[half].sum(axis=0, keepdims=True)
            for j in range(4):
                nrm[layer * 8 + half * 4 + j : layer * 8 + half * 4 + j + 1, :] = row[:, j * LANE : (j + 1) * LANE]

    zeros = (jnp.zeros((8, 512), F32), jnp.zeros((8, 512), F32))

    def second_body(i, sums):
        for h in range(2):
            start = pl.multiple_of(i * 64 + h * 32, 32)
            out, sums = norm_back(gh[pl.ds(start, 32), :], gain1, xhat1, der1, rstd1, start, 32, sums)
            gf[pl.ds(start, 32), :] = out.astype(BF)
        return sums

    sums1 = lax.fori_loop(0, 4, second_body, zeros)
    put_norm(1, sums1)
    grad_second = gf[pl.ds(0, 256), :]
    for h in range(2):
        gh[pl.ds(h * 256, 256), :] = dot(grad_second, wv[1, pl.ds(h * 512, 512), :], NT).astype(BF).astype(F32)

    def forward_frames():
        await_bytes(frecv.at[low, down], fg_r.at[0])
        launch(remote(frecv.at[low, down], frecv.at[low, down], fg_s.at[4], fg_r.at[4], (dp, up)))
        await_bytes(frecv.at[high, up], fg_r.at[1])
        launch(remote(frecv.at[high, up], frecv.at[high, up], fg_s.at[5], fg_r.at[5], (dp, down)))

    def kernel_grad(layer, left, sem):
        for half in range(2):
            right = gf[0 : left.shape[1], half * 256 : half * 256 + 256]
            for h in range(4):
                part = dot(left[h * 256 : (h + 1) * 256, :], right).astype(BF)
                for j in range(2):
                    convp[layer, 2 * half + j, h] = part[:, j * LANE : (j + 1) * LANE].reshape(4, 2, 4, 8, LANE)
            for j in (2 * half, 2 * half + 1):
                launch(remote(convp.at[layer, j, :, :, 1 - c], convr.at[layer, j], rs_s.at[sem + j, 3], rs_r.at[sem + j], mate))

    kernel_grad(1, hidt, 0)

    def conv_core(layer, j, sem):
        await_bytes(convr.at[layer, j], rs_r.at[sem])
        convb[layer, j] = (
            convp[layer, j, :, :, c].astype(F32) + convr[layer, j].astype(F32)
        ).astype(BF)

    base = ("z", "x", "y")
    plane = sorted([(i, j) for i in range(4) for j in range(4) if i or j], key=lambda one: one.count(2) * 5 + 4 - one.count(0), reverse=True)

    def conv_send(layer, j, sem):
        scatter(convb, conv1, (layer, j), base, ("x", "z")[j % 2], sem)

    def conv_take(layer, j, sem):
        total = gather(convb, conv1, (layer, j), base, ("x", "z")[j % 2], sem)
        convb1[j % 2, :, :, layer, j // 2] = total.astype(BF)

    def plane_peer(axis, i, j):
        if axis == "z":
            return (dp_of((z + i) % 4, x, c), (y + j) % 4)
        return (dp_of(z, (x + i) % 4, c), (y + j) % 4)

    def conv_last_send(p):
        axis = ("z", "x")[p]
        for n, (i, j) in enumerate(plane):
            launch(
                remote(
                    convb1.at[p, (sizes[axis] + i) % 4, (y + j) % 4],
                    conv2.at[p, n],
                    pl_s.at[p, n],
                    pl_r.at[p],
                    plane_peer(axis, i, j),
                )
            )

    def conv_last_take(p):
        await_bytes(conv2.at[p], pl_r.at[p])
        total = convb1[p, sizes[("z", "x")[p]], y].astype(F32)
        for n in range(15):
            total = total + conv2[p, n].astype(F32)
        for layer in range(2):
            for j in range(2):
                at = 2 * j + p
                gconv_out[layer, :, at * LANE : (at + 1) * LANE] = total[layer, j]

    def first_body(i, sums):
        for h in range(2):
            start = pl.multiple_of(i * 64 + h * 32, 32)
            out, sums = norm_back(gh[pl.ds(start, 32), :], gain0, xhat0, der0, rstd0, start, 32, sums)
            gf[pl.ds(start, 32), :] = out.astype(BF)
        return sums

    sums0 = lax.fori_loop(0, 8, first_body, zeros)
    put_norm(0, sums0)
    to_mate = remote(nrm, nrmr, nm_s.at[0, 0], nm_r.at[0], mate)
    to_mate.start()

    for j in range(4):
        conv_core(1, j, j)
        conv_send(1, j, 16 + j)
    kernel_grad(0, actt, 8)
    forward_frames()
    await_bytes(nrmr, nm_r.at[0])
    to_mate.wait_send()
    nrm[...] = nrm[...] + nrmr[...]
    moving = []
    for k in range(1, 4):
        moving.append(remote(nrm, nrm1.at[k - 1], nm_s.at[1, k - 1], nm_r.at[1], peer("x", k)))
        moving[-1].start()
    for j in range(4):
        conv_core(0, j, 8 + j)
        conv_send(0, j, 20 + j)

    for h in range(2):
        gx[pl.ds(h * 256, 256), :] = dot(gf[pl.ds(h * 256, 256), :], wv[0], NT)

    @pl.loop(0, 8)
    def _(i):
        for h in range(2):
            rows = gx[pl.ds(pl.multiple_of(h * 256 + i * 32, 32), 32), :]
            for k in range(2):
                for j in range(4):
                    xo[j, pl.ds(2 * h + k, 32, stride=4), :] = rows[:, k * 512 + j * LANE : k * 512 + (j + 1) * LANE]
        out = jnp.concatenate([xo[j] for j in range(4)], axis=1)
        gfeat_out[pl.ds(pl.multiple_of(i * 128, 128), 128), :] = out.astype(BF)

    for j in range(4):
        conv_take(1, j, 16 + j)
    await_bytes(nrm1, nm_r.at[1])
    for one in moving:
        one.wait_send()
    nrm[...] = nrm[...] + nrm1[0] + nrm1[1] + nrm1[2]
    for n, (i, j) in enumerate(plane):
        launch(remote(nrm, nrm2.at[n], pl_s.at[2, n], pl_r.at[2], plane_peer("z", i, j)))

    await_bytes(frecv.at[high, down], fg_r.at[2])
    await_bytes(frecv.at[low, up], fg_r.at[3])
    await_bytes(frecv.at[low, far], fg_r.at[4])
    await_bytes(frecv.at[high, far], fg_r.at[5])
    packin[...] = dot(frecv[...].reshape(1024, 512), query[...], TN).astype(BF)
    part = dot(packin[...], gpv[...], NT).astype(BF)
    projp[...] = part.reshape(4, 4, 2, 16, WIDE)
    launch(remote(projp.at[:, :, 1 - c], projr, rs_s.at[4, 3], rs_r.at[4], mate))
    packed_out[...] = dot(pall[y, pl.ds(0, 320), :], packin[...]).astype(BF)
    for j in (0, 2):
        conv_take(0, j, 20 + j)
    conv_last_send(0)
    for j in (1, 3):
        conv_take(0, j, 20 + j)
    conv_last_send(1)
    await_bytes(projr, rs_r.at[4])
    projb[...] = (projp[:, :, c].astype(F32) + projr[...].astype(F32)).astype(BF)
    for n, (i, j) in enumerate(plane):
        launch(
            remote(
                projb.at[(z + i) % 4, (x + j) % 4],
                proj1.at[n],
                pl_s.at[3, n],
                pl_r.at[3],
                (dp_of((z + i) % 4, (x + j) % 4, c), y),
            )
        )
    await_bytes(nrm2, pl_r.at[2])
    total = nrm[...]
    for n in range(15):
        total = total + nrm2[n]
    gnorm_out[...] = total
    for p in range(2):
        conv_last_take(p)
    await_bytes(proj1, pl_r.at[3])
    total = projb[z, x].astype(F32)
    for n in range(15):
        total = total + proj1[n].astype(F32)
    gproj_out[...] = total[:, 0:320]

    for one in sends:
        one.wait_send()
    await_bytes(gsend.at[pl.ds(0, 127)], a2a_s.at[0])
    await_bytes(fsend.at[pl.ds(0, 31)], a2a_s.at[1])


def finish(
    packed_in, gfeat_in, gconv_in, gproj_in, gnorm_in, packed_out, gfeat_out, gconv_out, gproj_out, gnorm_out, sem
):
    copies = [
        pltpu.make_async_copy(packed_in, packed_out, sem.at[0]),
        pltpu.make_async_copy(gfeat_in, gfeat_out, sem.at[1]),
        pltpu.make_async_copy(gconv_in, gconv_out, sem.at[2]),
        pltpu.make_async_copy(gproj_in, gproj_out, sem.at[3]),
    ]
    for one in (1, 0, 2, 3):
        copies[one].start()
    d = lax.axis_index("dp") * 4 + lax.axis_index("mp")
    for layer in range(2):
        row = gnorm_in[pl.ds(layer * 8 + d // 16, 1), :]
        turned = pltpu.roll(row, LANE - (d % 16) * 8, 1)
        gnorm_out[layer : layer + 1, :] = turned[:, 0:8]
    for one in copies:
        one.wait()


def local(features, lengths, dests, offsets, conv_weight, norm_gain, norm_shift, proj_weight, grad_packed):
    vmem = pl.BlockSpec(memory_space=pltpu.VMEM)
    hbm = pl.BlockSpec(memory_space=pltpu.HBM)
    smem = pl.BlockSpec(memory_space=pltpu.SMEM)
    V = pltpu.VMEM
    D = pltpu.SemaphoreType.DMA
    scratch = [
        V((1024, 512), BF), V((2, 1024, 512), BF), V((WIDE, 512), BF), V((4, 128, LANE), F32),
        V((512, 1024), BF), V((1024, 512), BF), V((512, 512), F32), V((512, 512), F32), V((512, 512), F32), V((512, LANE), F32),
        V((256, 512), F32), V((256, 512), F32), V((256, LANE), F32),
        V((256, 1024), BF), V((1024, 256), BF), V((256, 512), BF),
        V((4, 4, 8, 1, LANE), F32), V((1024, 512), BF), V((128, 8, WIDE), BF), V((4, 32, 8, WIDE), BF),
        V((32, 8, 512), BF), V((32, 4, 8, 512), BF), V((4, WIDE, 512), BF), V((512, 512), BF),
        V((512, 512), F32), V((512, 512), BF), V((512, 1024), F32), V((4, 128, LANE), F32),
        V((2, 4, 4, 4, 2, 4, 8, LANE), BF), V((2, 4, 4, 4, 4, 8, LANE), BF), V((2, 4, 4, 4, 4, 8, LANE), BF),
        V((2, 4, 3, 4, 4, 8, LANE), BF), V((2, 4, 4, 2, 2, 8, LANE), BF), V((2, 15, 2, 2, 8, LANE), BF),
        V((4, 4, 2, 16, WIDE), BF), V((4, 4, 16, WIDE), BF), V((4, 4, 16, WIDE), BF), V((15, 16, WIDE), BF),
        V((16, LANE), F32), V((16, LANE), F32), V((3, 16, LANE), F32), V((15, 16, LANE), F32),
        D((4,)), D((13,)), D((3,)), D((7,)), D((7,)), D((2,)), D((2,)), D((6,)), D((6,)), D((24, 4)), D((24,)), D((2, 3)), D((2,)), D((4, 15)), D((4,)),
    ]
    results = ((320, 512), BF), ((1024, 512), BF), ((2, 8, 512), F32), ((16, 320), F32), ((16, LANE), F32)
    middle = pl.pallas_call(
        kernel,
        out_shape=tuple(pltpu.VMEM(*one) for one in results),
        in_specs=[smem] * 3 + [vmem] * 2 + [hbm] * 4,
        out_specs=(vmem,) * 5,
        scratch_shapes=scratch,
        compiler_params=pltpu.CompilerParams(collective_id=0, has_side_effects=True, vmem_limit_bytes=65_400_000),
    )(
        lengths, dests, offsets, norm_gain, norm_shift, features.reshape(1024, 512), conv_weight,
        proj_weight.T, grad_packed.T,
    )
    shapes = (*results[:4], ((2, 8), F32))
    packed, gfeat, gconv, gproj, gnorm = pl.pallas_call(
        finish,
        out_shape=tuple(jax.ShapeDtypeStruct(*one) for one in shapes),
        in_specs=[vmem] * 5,
        out_specs=(hbm, hbm, hbm, hbm, vmem),
        scratch_shapes=[D((4,))],
    )(*[pltpu.with_memory_space_constraint(one, pltpu.VMEM) for one in middle])
    return packed.T, gfeat.reshape(32, 32, 512), gconv, gnorm, gproj


def solution(mesh):
    return jax.shard_map(
        local,
        mesh=mesh,
        in_specs=(
            P(("dp", "mp"), None, None),
            P(("dp", "mp")),
            P(("dp", "mp")),
            P(("dp", "mp")),
            P(),
            P(),
            P(),
            P(None, "mp"),
            P("dp", "mp"),
        ),
        out_specs=(
            P("dp", "mp"),
            P(("dp", "mp"), None, None),
            P(None, ("dp", "mp"), None),
            P(None, ("dp", "mp")),
            P("dp", "mp"),
        ),
        check_vma=False,
    )
```

time: 66.3 us -> 54.1 us (0.82)
  the two profiles are of different devices: /device:TPU:0 before, /device:TPU:1 now
where the time goes in v3:
time: 54.1 us; the launch traced here: 54 us
  Pallas kernels  53.3 us (99%)
  between operations  0.64 us (1%)
    pallas_call x1, Pallas kernels, local(): pl.pallas_call(kernel, out_shape=tuple((pltpu.VMEM(*one) for one in resul...  51.6 us
    pallas_call x1, Pallas kernels, local(): pl.pallas_call(finish, out_shape=tuple((jax.ShapeDtypeStruct(*one) for on...  1.69 us

profile of v3, /device:TPU:1, one launch (start us, length us, event | category | flops | bytes accessed | tf_op | source)
XLA Modules:
  0.0 54.0 jit_solution(1541712886230260327)
XLA Ops:
  0.6 51.6 %shard_map.128 = (bf16[320,512]{1,0:T(8,128)(2,1)S(1)}, bf16[1024,512]{1,0:T(8,128)(2,1)S(1)}, f32[2,8,512]{2,1,0:T(8,128)S(1)}, f32[16,320]{1,0:T(8,128)S(1)}, f32[16,128]{1,0:T(8,128)S(1)}) custom-call(s32[32]{0:T(128)} %len_ref.1, s32[32]{0:T(128)} %dest_ref.1, s32[32]{0:T(128)} %off_ref.1, f32[2,512]{1,0:T(2,128)} %gain_ref.1, f32[2,512]{1,0:T(2,128)} %shift_ref.1, ...), custom_call_target="tpu_custom_call" | custom-call | tf_op jit(solution)/shard_map/pallas_call | solution.py:491
  52.3 1.7 %shard_map.129 = (bf16[320,512]{1,0:T(8,128)(2,1)}, bf16[1024,512]{1,0:T(8,128)(2,1)}, f32[2,8,512]{2,1,0:T(8,128)}, f32[16,320]{1,0:T(8,128)}, f32[2,8]{1,0:T(2,128)}) custom-call(bf16[320,512]{1,0:T(8,128)(2,1)S(1)} %get-tuple-element.15.packed_in, bf16[1024,512]{1,0:T(8,128)(2,1)S(1)} %get-tuple-element.16.gfeat_in, ...), custom_call_target="tpu_custom_call" | custom-call | tf_op jit(solution)/shard_map/pallas_call | solution.py:503

commit v4 on v3

v4 whole, which is shorter than its diff:
```python
import jax
import jax.numpy as jnp
from jax import lax
from jax.experimental import pallas as pl
from jax.experimental.pallas import tpu as pltpu
from jax.sharding import PartitionSpec as P

EPSILON = 1e-05
BF = jnp.bfloat16
F32 = jnp.float32
MESH = pl.DeviceIdType.MESH
NN = (((1,), (0,)), ((), ()))
NT = (((1,), (1,)), ((), ()))
TN = (((0,), (0,)), ((), ()))
LANE = 128
WIDE = 384


def dot(a, b, dims=NN):
    return lax.dot_general(a, b, dims, preferred_element_type=F32)


def iota(shape, dim):
    return lax.broadcasted_iota(jnp.int32, shape, dim)


def kernel(
    len_hbm, dest_hbm, off_hbm, gain_hbm, shift_hbm, feat_hbm, weight_hbm, proj_hbm, gp_hbm,
    packed_out, gfeat_out, gconv_out, gproj_out, gnorm_out,
    len_ref, dest_ref, off_ref, gain_ref, shift_ref, xb, wv, gpv, gpe, xf, act, actt, placet, pre, xhat0, der0, rstd0, xhat1, der1, rstd1, hid, hidt, frm,
    tbl, query, gsendb, gsends, gbig, gsmall, fsend, frecv, pall, packin,
    gh, gf, gx, xo,
    convp, convr, convb, conv1, convb1, conv2,
    projp, projr, projb, proj1,
    nrm, nrmr, nrm1, nrm2,
    in_sem, idx_s, idx_r, ag_s, ag_r, g_s, g_r, a2a_s, a2a_r, fg_s, fg_r, rs_s, rs_r, nm_s, nm_r, pl_s, pl_r,
):
    dp = lax.axis_index("dp")
    y = lax.axis_index("mp")
    z, q = dp // 8, dp % 8
    x, c = q // 2, q % 2
    odd = y % 2
    mine = (y // 2, pl.multiple_of(odd * 320, 64))

    def dp_of(zz, xx, cc):
        return zz * 8 + xx * 2 + cc

    def remote(src, dst, ssem, rsem, to):
        return pltpu.make_async_remote_copy(
            src_ref=src, dst_ref=dst, send_sem=ssem, recv_sem=rsem, device_id=to, device_id_type=MESH
        )

    def await_bytes(ref, sem):
        pltpu.make_async_copy(ref, ref, sem).wait()

    loads = [
        pltpu.make_async_copy(feat_hbm, xb, in_sem.at[0]),
        pltpu.make_async_copy(weight_hbm, wv, in_sem.at[1]),
        pltpu.make_async_copy(proj_hbm, pall.at[mine[0], pl.ds(mine[1], 320)], in_sem.at[2]),
        pltpu.make_async_copy(gp_hbm, gpv.at[pl.ds(0, 320)], in_sem.at[3]),
        pltpu.make_async_copy(gp_hbm, gpe.at[pl.ds(pl.multiple_of(odd * 64, 64), 320)], in_sem.at[4]),
    ]
    partners = (
        [(dp, (y + k) % 4) for k in range(1, 4)]
        + [(z * 8 + (q + k) % 8, y) for k in range(1, 8)]
        + [(((z + k) % 4) * 8 + q, y) for k in range(1, 4)]
    )
    barrier = pltpu.get_barrier_semaphore()
    for to in partners:
        pl.semaphore_signal(barrier, inc=1, device_id=to, device_id_type=MESH)
    small = [
        pltpu.make_async_copy(source, target, in_sem.at[5 + n])
        for n, (source, target) in enumerate(
            ((len_hbm, len_ref), (dest_hbm, dest_ref), (off_hbm, off_ref), (gain_hbm, gain_ref), (shift_hbm, shift_ref))
        )
    ]
    for one in small:
        one.start()
    for one in (0, 2, 4, 1, 3):
        loads[one].start()
    for one in small:
        one.wait()

    lane = iota((1, LANE), 1)
    row = jnp.full((1, LANE), 64, jnp.int32)
    for p in range(16):
        row = jnp.where(lane == dest_ref[2 * p], off_ref[2 * p] >> 3, row)
    tbl[y, z, q] = row.astype(F32)
    lane = iota((1, 256), 1)
    utterance, step = lane >> 3, lane & 7
    target = jnp.full((1, 256), -1, jnp.int32)
    for u in range(32):
        at = jnp.where(step < len_ref[u], dest_ref[u] * 8 + (off_ref[u] & 7) + step, -1)
        target = jnp.where(utterance == u, at, target)
    place = (iota((256, 256), 0) == target).astype(F32).astype(BF)

    gpv[pl.ds(320, 64), :] = jnp.zeros((64, 512), BF)

    loads[0].wait()

    @pl.loop(0, 8)
    def _(i):
        rows = xb[pl.ds(pl.multiple_of(i * 128, 128), 128), :].astype(F32)
        for j in range(4):
            xf[j] = rows[:, j * LANE : (j + 1) * LANE]
        for k in range(4):
            part = jnp.concatenate([xf[j, pl.ds(k, 32, stride=4), :] for j in range(4)], axis=1)
            act[pl.ds(pl.multiple_of((k // 2) * 256 + i * 32, 32), 32), (k % 2) * 512 : (k % 2) * 512 + 512] = part.astype(BF)

    pl.semaphore_wait(barrier, len(partners))

    sends = []

    def launch(copy):
        copy.start()

    def sent(ref, sem):
        sends.append((ref, sem))

    for k in range(1, 4):
        launch(remote(tbl.at[y, z, q], tbl.at[y, z, q], idx_s.at[0], idx_r.at[0], (((z + k) % 4) * 8 + q, y)))
    loads[2].wait()
    up, down, far = (y + 1) % 4, (y + 3) % 4, (y + 2) % 4

    def shard(yy, start, count):
        at = pl.multiple_of((yy % 2) * 320 + start, 16)
        return pall.at[yy // 2, pl.ds(at, count)]

    own = c * 160
    launch(remote(shard(y, own, 160), shard(y, own, 160), ag_s.at[0], ag_r.at[0], (dp, up)))
    launch(remote(shard(y, own, 160), shard(y, own, 160), ag_s.at[0], ag_r.at[1], (dp, down)))
    sent(pall.at[0, pl.ds(0, 320)], ag_s.at[0])
    loads[4].wait()
    edge = gpe.at[pl.ds(pl.multiple_of(256 - 192 * odd, 64), 64)]
    launch(remote(edge, gpe.at[pl.ds(pl.multiple_of(320 * odd, 64), 64)], ag_s.at[3], ag_r.at[4], (dp, y + 1 - 2 * odd)))
    sent(edge, ag_s.at[3])

    loads[1].wait()
    pre[...] = dot(act[...], wv[0])

    await_bytes(tbl.at[y, pl.ds(0, 3), 0], idx_r.at[0])
    sent(tbl.at[y, pl.ds(0, 3), 0], idx_s.at[0])
    for k in range(1, 8):
        launch(remote(tbl.at[y, :, q], tbl.at[y, :, q], idx_s.at[1], idx_r.at[1], (z * 8 + (q + k) % 8, y)))

    def norm_gelu(source, gain, shift, xhat, der, rstd, start, count):
        v = source[pl.ds(start, count), :]
        mean = jnp.mean(v, axis=-1, keepdims=True)
        centred = v - mean
        spread = jnp.mean(centred * centred, axis=-1, keepdims=True)
        inv = lax.rsqrt(spread + EPSILON)
        normal = centred * inv
        arg = normal * gain + shift
        cdf = 0.5 + 0.5 * lax.erf(arg * (2.0**-0.5))
        xhat[pl.ds(start, count), :] = normal
        der[pl.ds(start, count), :] = cdf + arg * (jnp.exp(-0.5 * arg * arg) * 0.3989422804014327)
        rstd[pl.ds(start, count), :] = jnp.broadcast_to(inv, (count, LANE))
        return arg * cdf

    gain0, shift0 = gain_ref[0:1, :], shift_ref[0:1, :]
    gain1, shift1 = gain_ref[1:2, :], shift_ref[1:2, :]

    def first_rows(lo, hi):
        @pl.loop(lo, hi)
        def _(i):
            start = pl.multiple_of(i * 32, 32)
            for h in range(2):
                out = norm_gelu(pre, gain0, shift0, xhat0, der0, rstd0, pl.multiple_of(start + h * 256, 32), 32)
                hid[pl.ds(start, 32), h * 512 : (h + 1) * 512] = out.astype(BF)

    first_rows(0, 8)
    pre[pl.ds(0, 256), :] = dot(hid[...], wv[1])

    @pl.loop(0, 4)
    def _(i):
        for h in range(2):
            start = pl.multiple_of(i * 64 + h * 32, 32)
            out = norm_gelu(pre, gain1, shift1, xhat1, der1, rstd1, start, 32)
            frm[pl.ds(start, 32), :] = out.astype(BF)

    fsend[...] = dot(place, frm[...]).astype(BF).reshape(32, 8, 512)

    await_bytes(tbl.at[y, :, pl.ds(0, 7)], idx_r.at[1])
    sent(tbl.at[y, :, pl.ds(0, 7)], idx_s.at[1])
    for k in range(1, 4):
        launch(remote(tbl.at[y], tbl.at[y], idx_s.at[2], idx_r.at[2], (dp, (y + k) % 4)))
    own_f = pltpu.make_async_copy(fsend.at[dp], frecv.at[dp, y], a2a_r.at[0])
    own_f.start()

    @pl.loop(1, 32)
    def _(k):
        to = (dp + k) % 32
        remote(fsend.at[to], frecv.at[dp, y], a2a_s.at[0], a2a_r.at[0], (to, y)).start()

    await_bytes(shard(down, own, 160), ag_r.at[0])
    launch(remote(shard(down, own, 80), shard(down, own, 80), ag_s.at[1], ag_r.at[2], (dp, up)))
    await_bytes(shard(up, own, 160), ag_r.at[1])
    launch(remote(shard(up, own + 80, 80), shard(up, own + 80, 80), ag_s.at[1], ag_r.at[2], (dp, down)))
    sent(shard(y, 0, 160), ag_s.at[1])

    loads[3].wait()
    await_bytes(tbl.at[pl.ds(0, 3)], idx_r.at[2])
    sent(tbl.at[pl.ds(0, 3)], idx_s.at[2])
    table = jnp.concatenate([tbl[m].reshape(32, LANE) for m in range(4)], axis=0).astype(BF)
    pick = (iota((128, 512), 0) == dp).astype(F32).astype(BF)
    blocks = dot(table, pick).astype(BF)
    row_id = iota((128, 512), 0)
    column = (iota((128, 512), 1) - (row_id & 7)).astype(F32)
    slot = iota((128, 128), 0) >> 3
    wanted = (slot & 3) * 32 + (slot >> 2) * 2
    await_bytes(gpe.at[pl.ds(0, 64)], ag_r.at[4])

    for turn in (2, 1, 3, 0):
        part = (z + turn) % 4
        for kind in range(2):
            core = odd if kind == 0 else 1 - odd
            spread = (wanted + part * 8 + core == iota((128, 128), 1)).astype(F32).astype(BF)
            one_hot = (dot(spread, blocks) * 8.0 == column).astype(F32).astype(BF)
            if kind == 0:
                values = dot(one_hot, gpe[...], NT)
                gsendb[pl.ds(part * 16, 16)] = values.astype(BF).reshape(16, 8, 384)
            else:
                values = dot(one_hot, gpe[pl.ds(pl.multiple_of(128 * odd, 128), 256), :], NT)
                gsends[pl.ds(part * 16, 16)] = values.astype(BF).reshape(16, 8, 256)
        for along in (2, 1, 3, 0):
            for across in (2, 1, 3, 0):
                side = (y + across) % 4
                column_x = (x + along) % 4
                for kind, (source, landing) in enumerate(((gsendb, gbig), (gsends, gsmall))):
                    core = odd if kind == 0 else 1 - odd
                    src = source.at[part * 16 + column_x * 4 + side]
                    dst = landing.at[y // 2, dp]
                    copy = remote(src, dst, g_s.at[kind], g_r.at[kind], (dp_of(part, column_x, core), side))
                    if turn or along or across:
                        copy.start()
                    else:
                        pl.when(core != c)(copy.start)
                        pl.when(core == c)(pltpu.make_async_copy(src, dst, g_r.at[kind]).start)

    await_bytes(shard(far, own, 160), ag_r.at[2])
    mate = (dp_of(z, x, 1 - c), y)
    for at in (up, down, far):
        launch(remote(shard(at, own, 160), shard(at, own, 160), ag_s.at[2], ag_r.at[3], mate))
    sent(pall.at[0, pl.ds(0, 480)], ag_s.at[2])

    placet[...] = place.T
    for part in range(4):
        slot = (iota((256, 128), 0) >> 3) + part * 32
        spread = ((slot & 3) * 32 + (slot >> 2) == iota((256, 128), 1)).astype(F32).astype(BF)
        column = (iota((256, 512), 1) - (iota((256, 512), 0) & 7)).astype(F32)
        query[part * 256 : part * 256 + 256, :] = (dot(spread, blocks) * 8.0 == column).astype(F32).astype(BF)
    actt[...] = act[...].T
    hidt[...] = hid[...].T
    await_bytes(pall.at[0, pl.ds(0, 480)], ag_r.at[3])
    await_bytes(frecv.at[:, 0], a2a_r.at[0])
    low, high = pl.ds(0, 16), pl.ds(16, 16)
    for n, (to, half) in enumerate(((up, low), (down, high), (up, high), (down, low))):
        launch(remote(frecv.at[half, y], frecv.at[half, y], fg_s.at[0], fg_r.at[min(n, 2)], (dp, to)))
    sent(frecv.at[low], fg_s.at[0])
    await_bytes(gbig, g_r.at[0])
    await_bytes(gsmall, g_r.at[1])

    total = None
    for m in range(2):
        part = dot(gbig[m].reshape(256, 384), pall[m, pl.ds(pl.multiple_of(256 * c, 128), 384), :])
        total = part if total is None else total + part
        total = total + dot(gsmall[m].reshape(256, 256), pall[m, pl.ds(pl.multiple_of(384 - 384 * c, 128), 256), :])
    grad_frames = dot(placet[...], total.astype(BF))
    gh[pl.ds(0, 256), :] = grad_frames

    sizes = dict(x=x, y=y, z=z)

    def peer(axis, k):
        if axis == "x":
            return (dp_of(z, (x + k) % 4, c), y)
        if axis == "z":
            return (dp_of((z + k) % 4, x, c), y)
        return (dp, (y + k) % 4)

    def chunk(ref, lead, dims, axis, at):
        pos = dims.index(axis)
        return ref.at[tuple(lead) + (slice(None),) * pos + (at,)]

    def scatter(source, landing, lead, dims, axis, send, sem):
        for k in range(1, 4):
            at = (sizes[axis] + k) % 4
            launch(
                remote(
                    chunk(source, lead, dims, axis, at),
                    landing.at[tuple(lead) + (k - 1,)],
                    rs_s.at[send],
                    rs_r.at[sem],
                    peer(axis, k),
                )
            )

    def gather(source, landing, lead, dims, axis):
        total = chunk(source, lead, dims, axis, sizes[axis])[...].astype(F32)
        for k in range(3):
            total = total + landing[tuple(lead) + (k,)].astype(F32)
        return total

    def norm_back(upstream, gain, xhat, der, rstd, start, count, sums):
        dy = upstream * der[pl.ds(start, count), :]
        normal = xhat[pl.ds(start, count), :]
        dyn = dy * normal
        dg = sums[0] + dyn.reshape(count // 8, 8, 512).sum(axis=0)
        ds = sums[1] + dy.reshape(count // 8, 8, 512).sum(axis=0)
        mean_d = jnp.mean(dy * gain, axis=-1, keepdims=True)
        mean_dn = jnp.mean(dyn * gain, axis=-1, keepdims=True)
        inv = rstd[pl.ds(start, count), :][:, 0:1]
        return inv * (dy * gain - mean_d - normal * mean_dn), (dg, ds)

    def put_norm(layer, sums):
        for half in range(2):
            row = sums[half].sum(axis=0, keepdims=True)
            for j in range(4):
                nrm[layer * 8 + half * 4 + j : layer * 8 + half * 4 + j + 1, :] = row[:, j * LANE : (j + 1) * LANE]

    zeros = (jnp.zeros((8, 512), F32), jnp.zeros((8, 512), F32))

    def second_body(i, sums):
        for h in range(2):
            start = pl.multiple_of(i * 64 + h * 32, 32)
            out, sums = norm_back(gh[pl.ds(start, 32), :], gain1, xhat1, der1, rstd1, start, 32, sums)
            gf[pl.ds(start, 32), :] = out.astype(BF)
        return sums

    sums1 = lax.fori_loop(0, 4, second_body, zeros)
    put_norm(1, sums1)
    grad_second = gf[pl.ds(0, 256), :]
    for h in range(2):
        gh[pl.ds(h * 256, 256), :] = dot(grad_second, wv[1, pl.ds(h * 512, 512), :], NT).astype(BF).astype(F32)

    def forward_frames():
        await_bytes(frecv.at[low, down], fg_r.at[0])
        launch(remote(frecv.at[low, down], frecv.at[low, down], fg_s.at[1], fg_r.at[2], (dp, up)))
        await_bytes(frecv.at[high, up], fg_r.at[1])
        launch(remote(frecv.at[high, up], frecv.at[high, up], fg_s.at[1], fg_r.at[2], (dp, down)))
        sent(frecv.at[:, y], fg_s.at[1])

    def kernel_grad(layer, left):
        for half in range(2):
            right = gf[0 : left.shape[1], half * 256 : half * 256 + 256]
            for h in range(4):
                part = dot(left[h * 256 : (h + 1) * 256, :], right).astype(BF)
                for j in range(2):
                    convp[layer, 2 * half + j, h] = part[:, j * LANE : (j + 1) * LANE].reshape(4, 2, 4, 8, LANE)
            for j in (2 * half, 2 * half + 1):
                launch(remote(convp.at[layer, j, :, :, 1 - c], convr.at[layer, j], rs_s.at[layer], rs_r.at[2 * layer + half], mate))
        sent(convr.at[layer], rs_s.at[layer])

    kernel_grad(1, hidt)
    forward_frames()

    def conv_core(layer, j):
        if j % 2 == 0:
            await_bytes(convr.at[layer, pl.ds(j, 2)], rs_r.at[2 * layer + j // 2])
        convb[layer, j] = (
            convp[layer, j, :, :, c].astype(F32) + convr[layer, j].astype(F32)
        ).astype(BF)

    base = ("z", "x", "y")
    plane = sorted([(i, j) for i in range(4) for j in range(4) if i or j], key=lambda one: one.count(2) * 5 + 4 - one.count(0), reverse=True)

    conv_axis = (("x", "z", "y", "y"), ("x", "z", "x", "z"))
    groups = {
        axis: [(layer, j) for layer in range(2) for j in range(4) if conv_axis[layer][j] == axis] for axis in "xyz"
    }
    order = "xyz"

    def others_of(axis):
        return tuple(one for one in base if one != axis)

    def conv_send(layer, j):
        scatter(convb, conv1, (layer, j), base, conv_axis[layer][j], 3 + layer, 5 if layer else 6 + j)
        if j == 3:
            sent(conv1.at[layer], rs_s.at[3 + layer])

    def conv_take(layer, j):
        axis = conv_axis[layer][j]
        if layer == 0:
            await_bytes(conv1.at[layer, j], rs_r.at[6 + j])
        elif j == 0:
            await_bytes(conv1.at[layer], rs_r.at[5])
        total = gather(convb, conv1, (layer, j), base, axis)
        convb1[order.index(axis), :, :, groups[axis].index((layer, j))] = total.astype(BF)

    def plane_peer(first, second, i, j):
        at = dict(sizes)
        at[first] = (at[first] + i) % 4
        at[second] = (at[second] + j) % 4
        return (dp_of(at["z"], at["x"], c), at["y"])

    def conv_last_send(axis):
        p, count = order.index(axis), len(groups[axis])
        first, second = others_of(axis)
        for n, (i, j) in enumerate(plane):
            launch(
                remote(
                    convb1.at[p, (sizes[first] + i) % 4, (sizes[second] + j) % 4, pl.ds(0, count)],
                    conv2.at[p, n, pl.ds(0, count)],
                    pl_s.at[p],
                    pl_r.at[p],
                    plane_peer(first, second, i, j),
                )
            )
        sent(conv2.at[p, :, pl.ds(0, count)], pl_s.at[p])

    def conv_last_take(axis):
        p, count = order.index(axis), len(groups[axis])
        first, second = others_of(axis)
        await_bytes(conv2.at[p, :, pl.ds(0, count)], pl_r.at[p])
        total = convb1[p, sizes[first], sizes[second], 0:count].astype(F32)
        for n in range(15):
            total = total + conv2[p, n, 0:count].astype(F32)
        for at, (layer, j) in enumerate(groups[axis]):
            gconv_out[layer, :, j * LANE : (j + 1) * LANE] = total[at]

    def first_body(i, sums):
        for h in range(2):
            start = pl.multiple_of(i * 64 + h * 32, 32)
            out, sums = norm_back(gh[pl.ds(start, 32), :], gain0, xhat0, der0, rstd0, start, 32, sums)
            gf[pl.ds(start, 32), :] = out.astype(BF)
        return sums

    sums0 = lax.fori_loop(0, 8, first_body, zeros)
    put_norm(0, sums0)
    to_mate = remote(nrm, nrmr, nm_s.at[0], nm_r.at[0], mate)
    to_mate.start()

    for j in range(4):
        conv_core(1, j)
        conv_send(1, j)
    kernel_grad(0, actt)
    for h in range(2):
        gx[pl.ds(h * 256, 256), :] = dot(gf[pl.ds(h * 256, 256), :], wv[0], NT)
    await_bytes(nrmr, nm_r.at[0])
    to_mate.wait_send()
    nrm[...] = nrm[...] + nrmr[...]
    for k in range(1, 4):
        launch(remote(nrm, nrm1.at[k - 1], nm_s.at[1], nm_r.at[1], peer("x", k)))
    for j in range(4):
        conv_core(0, j)
        conv_send(0, j)

    @pl.loop(0, 8)
    def _(i):
        for h in range(2):
            rows = gx[pl.ds(pl.multiple_of(h * 256 + i * 32, 32), 32), :]
            for k in range(2):
                for j in range(4):
                    xo[j, pl.ds(2 * h + k, 32, stride=4), :] = rows[:, k * 512 + j * LANE : k * 512 + (j + 1) * LANE]
        out = jnp.concatenate([xo[j] for j in range(4)], axis=1)
        gfeat_out[pl.ds(pl.multiple_of(i * 128, 128), 128), :] = out.astype(BF)

    await_bytes(frecv.at[low], fg_r.at[2])
    packin[...] = dot(frecv[...].reshape(1024, 512), query[...], TN).astype(BF)
    part = dot(packin[...], gpv[...], NT).astype(BF)
    projp[...] = part.reshape(4, 4, 2, 16, WIDE)
    launch(remote(projp.at[:, :, 1 - c], projr, rs_s.at[2], rs_r.at[4], mate))
    sent(projr, rs_s.at[2])
    await_bytes(nrm1, nm_r.at[1])
    await_bytes(nrm1, nm_s.at[1])
    nrm[...] = nrm[...] + nrm1[0] + nrm1[1] + nrm1[2]
    for n, (i, j) in enumerate(plane):
        launch(remote(nrm, nrm2.at[n], pl_s.at[3], pl_r.at[3], plane_peer("z", "y", i, j)))
    sent(nrm2, pl_s.at[3])
    await_bytes(projr, rs_r.at[4])
    projb[...] = (projp[:, :, c].astype(F32) + projr[...].astype(F32)).astype(BF)
    for n, (i, j) in enumerate(plane):
        launch(
            remote(
                projb.at[(z + i) % 4, (x + j) % 4], proj1.at[n], pl_s.at[4], pl_r.at[4], plane_peer("z", "x", i, j)
            )
        )
    sent(proj1, pl_s.at[4])
    for j in range(4):
        conv_take(1, j)
    for axis in order:
        for j in range(4):
            if conv_axis[0][j] == axis:
                conv_take(0, j)
        conv_last_send(axis)
    packed_out[...] = dot(pall[mine[0], pl.ds(mine[1], 320), :], packin[...]).astype(BF)
    await_bytes(nrm2, pl_r.at[3])
    total = nrm[...]
    for n in range(15):
        total = total + nrm2[n]
    gnorm_out[...] = total
    await_bytes(proj1, pl_r.at[4])
    total = projb[z, x].astype(F32)
    for n in range(15):
        total = total + proj1[n].astype(F32)
    gproj_out[...] = total[:, 0:320]
    for axis in order:
        conv_last_take(axis)

    for ref, sem in sends:
        await_bytes(ref, sem)

    @pl.when(odd == c)
    def _():
        await_bytes(gsendb.at[pl.ds(0, 63)], g_s.at[0])
        await_bytes(gsends, g_s.at[1])

    @pl.when(odd != c)
    def _():
        await_bytes(gsendb, g_s.at[0])
        await_bytes(gsends.at[pl.ds(0, 63)], g_s.at[1])

    await_bytes(fsend.at[pl.ds(0, 31)], a2a_s.at[0])


def finish(
    packed_in, gfeat_in, gconv_in, gproj_in, gnorm_in, packed_out, gfeat_out, gconv_out, gproj_out, gnorm_out, sem
):
    copies = [
        pltpu.make_async_copy(packed_in, packed_out, sem.at[0]),
        pltpu.make_async_copy(gfeat_in, gfeat_out, sem.at[1]),
        pltpu.make_async_copy(gconv_in, gconv_out, sem.at[2]),
        pltpu.make_async_copy(gproj_in, gproj_out, sem.at[3]),
    ]
    for one in (1, 0, 2, 3):
        copies[one].start()
    d = lax.axis_index("dp") * 4 + lax.axis_index("mp")
    for layer in range(2):
        row = gnorm_in[pl.ds(layer * 8 + d // 16, 1), :]
        turned = pltpu.roll(row, LANE - (d % 16) * 8, 1)
        gnorm_out[layer : layer + 1, :] = turned[:, 0:8]
    for one in copies:
        one.wait()


def local(features, lengths, dests, offsets, conv_weight, norm_gain, norm_shift, proj_weight, grad_packed):
    vmem = pl.BlockSpec(memory_space=pltpu.VMEM)
    hbm = pl.BlockSpec(memory_space=pltpu.HBM)
    S = pltpu.SMEM
    V = pltpu.VMEM
    D = pltpu.SemaphoreType.DMA
    scratch = [
        S((32,), jnp.int32), S((32,), jnp.int32), S((32,), jnp.int32), V((2, 512), F32), V((2, 512), F32),
        V((1024, 512), BF), V((2, 1024, 512), BF), V((WIDE, 512), BF), V((WIDE, 512), BF), V((4, 128, LANE), F32),
        V((512, 1024), BF), V((1024, 512), BF), V((256, 256), BF), V((512, 512), F32), V((512, 512), F32), V((512, 512), F32), V((512, LANE), F32),
        V((256, 512), F32), V((256, 512), F32), V((256, LANE), F32),
        V((256, 1024), BF), V((1024, 256), BF), V((256, 512), BF),
        V((4, 4, 8, 1, LANE), F32), V((1024, 512), BF), V((64, 8, 384), BF), V((64, 8, 256), BF), V((2, 32, 8, 384), BF), V((2, 32, 8, 256), BF),
        V((32, 8, 512), BF), V((32, 4, 8, 512), BF), V((2, 640, 512), BF), V((512, 512), BF),
        V((512, 512), F32), V((512, 512), BF), V((512, 1024), F32), V((4, 128, LANE), F32),
        V((2, 4, 4, 4, 2, 4, 8, LANE), BF), V((2, 4, 4, 4, 4, 8, LANE), BF), V((2, 4, 4, 4, 4, 8, LANE), BF),
        V((2, 4, 3, 4, 4, 8, LANE), BF), V((3, 4, 4, 3, 8, LANE), BF), V((3, 15, 3, 8, LANE), BF),
        V((4, 4, 2, 16, WIDE), BF), V((4, 4, 16, WIDE), BF), V((4, 4, 16, WIDE), BF), V((15, 16, WIDE), BF),
        V((16, LANE), F32), V((16, LANE), F32), V((3, 16, LANE), F32), V((15, 16, LANE), F32),
        D((10,)), D((3,)), D((3,)), D((4,)), D((5,)), D((2,)), D((2,)), D((1,)), D((1,)), D((2,)), D((3,)), D((5,)), D((10,)),
        D((2,)), D((2,)), D((5,)), D((5,)),
    ]
    results = ((320, 512), BF), ((1024, 512), BF), ((2, 8, 512), F32), ((16, 320), F32), ((16, LANE), F32)
    middle = pl.pallas_call(
        kernel,
        out_shape=tuple(pltpu.VMEM(*one) for one in results),
        in_specs=[hbm] * 9,
        out_specs=(vmem,) * 5,
        scratch_shapes=scratch,
        compiler_params=pltpu.CompilerParams(collective_id=0, has_side_effects=True, vmem_limit_bytes=65_400_000),
    )(
        lengths, dests, offsets, norm_gain, norm_shift, features.reshape(1024, 512), conv_weight,
        proj_weight.T, grad_packed.T,
    )
    shapes = (*results[:4], ((2, 8), F32))
    packed, gfeat, gconv, gproj, gnorm = pl.pallas_call(
        finish,
        out_shape=tuple(jax.ShapeDtypeStruct(*one) for one in shapes),
        in_specs=[vmem] * 5,
        out_specs=(hbm, hbm, hbm, hbm, vmem),
        scratch_shapes=[D((4,))],
    )(*[pltpu.with_memory_space_constraint(one, pltpu.VMEM) for one in middle])
    return packed.T, gfeat.reshape(32, 32, 512), gconv, gnorm, gproj


def solution(mesh):
    return jax.shard_map(
        local,
        mesh=mesh,
        in_specs=(
            P(("dp", "mp"), None, None),
            P(("dp", "mp")),
            P(("dp", "mp")),
            P(("dp", "mp")),
            P(),
            P(),
            P(),
            P(None, "mp"),
            P("dp", "mp"),
        ),
        out_specs=(
            P("dp", "mp"),
            P(("dp", "mp"), None, None),
            P(None, ("dp", "mp"), None),
            P(None, ("dp", "mp")),
            P("dp", "mp"),
        ),
        check_vma=False,
    )
```

time: 54.1 us -> 49.4 us (0.913)
  Pallas kernels: 53.3 us -> 48.7 us
    pallas_call x1, Pallas kernels: 51.6 us -> 47 us  [local(): pl.pallas_call(kernel, out_shape=tuple((pltpu.VMEM(*one) for one in resul...]
where the time goes in v4:
time: 49.4 us; the launch traced here: 49.3 us
  Pallas kernels  48.7 us (99%)
  between operations  0.64 us (1%)
    pallas_call x1, Pallas kernels, local(): pl.pallas_call(kernel, out_shape=tuple((pltpu.VMEM(*one) for one in resul...  47 us
    pallas_call x1, Pallas kernels, local(): pl.pallas_call(finish, out_shape=tuple((jax.ShapeDtypeStruct(*one) for on...  1.69 us

profile of v4, /device:TPU:1, one launch (start us, length us, event | category | flops | bytes accessed | tf_op | source)
XLA Modules:
  0.0 49.3 jit_solution(5875516362579648767)
XLA Ops:
  0.6 47.0 %shard_map.128 = (bf16[320,512]{1,0:T(8,128)(2,1)S(1)}, bf16[1024,512]{1,0:T(8,128)(2,1)S(1)}, f32[2,8,512]{2,1,0:T(8,128)S(1)}, f32[16,320]{1,0:T(8,128)S(1)}, f32[16,128]{1,0:T(8,128)S(1)}) custom-call(s32[32]{0:T(128)} %len_hbm.1, s32[32]{0:T(128)} %dest_hbm.1, s32[32]{0:T(128)} %off_hbm.1, f32[2,512]{1,0:T(2,128)} %gain_hbm.1, f32[2,512]{1,0:T(2,128)} %shift_hbm.1, ...), custom_call_target="tpu_custom_call" | custom-call | tf_op jit(solution)/shard_map/pallas_call | solution.py:558
  47.6 1.7 %shard_map.129 = (bf16[320,512]{1,0:T(8,128)(2,1)}, bf16[1024,512]{1,0:T(8,128)(2,1)}, f32[2,8,512]{2,1,0:T(8,128)}, f32[16,320]{1,0:T(8,128)}, f32[2,8]{1,0:T(2,128)}) custom-call(bf16[320,512]{1,0:T(8,128)(2,1)S(1)} %get-tuple-element.15.packed_in, bf16[1024,512]{1,0:T(8,128)(2,1)S(1)} %get-tuple-element.16.gfeat_in, ...), custom_call_target="tpu_custom_call" | custom-call | tf_op jit(solution)/shard_map/pallas_call | solution.py:570

commit v5 on v4

--- a/solution.py
+++ b/solution.py
@@ -138,11 +138,6 @@
     loads[1].wait()
     pre[...] = dot(act[...], wv[0])
 
-    await_bytes(tbl.at[y, pl.ds(0, 3), 0], idx_r.at[0])
-    sent(tbl.at[y, pl.ds(0, 3), 0], idx_s.at[0])
-    for k in range(1, 8):
-        launch(remote(tbl.at[y, :, q], tbl.at[y, :, q], idx_s.at[1], idx_r.at[1], (z * 8 + (q + k) % 8, y)))
-
     def norm_gelu(source, gain, shift, xhat, der, rstd, start, count):
         v = source[pl.ds(start, count), :]
         mean = jnp.mean(v, axis=-1, keepdims=True)
@@ -168,7 +163,13 @@
                 out = norm_gelu(pre, gain0, shift0, xhat0, der0, rstd0, pl.multiple_of(start + h * 256, 32), 32)
                 hid[pl.ds(start, 32), h * 512 : (h + 1) * 512] = out.astype(BF)
 
-    first_rows(0, 8)
+    first_rows(0, 4)
+    await_bytes(tbl.at[y, pl.ds(0, 3), 0], idx_r.at[0])
+    sent(tbl.at[y, pl.ds(0, 3), 0], idx_s.at[0])
+    for k in range(1, 8):
+        launch(remote(tbl.at[y, :, q], tbl.at[y, :, q], idx_s.at[1], idx_r.at[1], (z * 8 + (q + k) % 8, y)))
+
+    first_rows(4, 8)
     pre[pl.ds(0, 256), :] = dot(hid[...], wv[1])
 
     @pl.loop(0, 4)
@@ -199,20 +200,19 @@
     sent(shard(y, 0, 160), ag_s.at[1])
 
     loads[3].wait()
+    await_bytes(gpe.at[pl.ds(0, 64)], ag_r.at[4])
+    pick = (iota((128, 512), 0) == dp).astype(F32).astype(BF)
+    column = (iota((128, 512), 1) - (iota((128, 512), 0) & 7)).astype(F32)
+    slot = iota((128, 128), 0) >> 3
+    wanted = (slot & 3) * 32 + (slot >> 2) * 2
     await_bytes(tbl.at[pl.ds(0, 3)], idx_r.at[2])
     sent(tbl.at[pl.ds(0, 3)], idx_s.at[2])
     table = jnp.concatenate([tbl[m].reshape(32, LANE) for m in range(4)], axis=0).astype(BF)
-    pick = (iota((128, 512), 0) == dp).astype(F32).astype(BF)
     blocks = dot(table, pick).astype(BF)
-    row_id = iota((128, 512), 0)
-    column = (iota((128, 512), 1) - (row_id & 7)).astype(F32)
-    slot = iota((128, 128), 0) >> 3
-    wanted = (slot & 3) * 32 + (slot >> 2) * 2
-    await_bytes(gpe.at[pl.ds(0, 64)], ag_r.at[4])
 
     for turn in (2, 1, 3, 0):
         part = (z + turn) % 4
-        for kind in range(2):
+        for kind, (source, landing) in enumerate(((gsendb, gbig), (gsends, gsmall))):
             core = odd if kind == 0 else 1 - odd
             spread = (wanted + part * 8 + core == iota((128, 128), 1)).astype(F32).astype(BF)
             one_hot = (dot(spread, blocks) * 8.0 == column).astype(F32).astype(BF)
@@ -222,12 +222,10 @@
             else:
                 values = dot(one_hot, gpe[pl.ds(pl.multiple_of(128 * odd, 128), 256), :], NT)
                 gsends[pl.ds(part * 16, 16)] = values.astype(BF).reshape(16, 8, 256)
-        for along in (2, 1, 3, 0):
-            for across in (2, 1, 3, 0):
-                side = (y + across) % 4
-                column_x = (x + along) % 4
-                for kind, (source, landing) in enumerate(((gsendb, gbig), (gsends, gsmall))):
-                    core = odd if kind == 0 else 1 - odd
+            for along in (2, 1, 3, 0):
+                for across in (2, 1, 3, 0):
+                    side = (y + across) % 4
+                    column_x = (x + along) % 4
                     src = source.at[part * 16 + column_x * 4 + side]
                     dst = landing.at[y // 2, dp]
                     copy = remote(src, dst, g_s.at[kind], g_r.at[kind], (dp_of(part, column_x, core), side))
@@ -460,12 +458,7 @@
     projp[...] = part.reshape(4, 4, 2, 16, WIDE)
     launch(remote(projp.at[:, :, 1 - c], projr, rs_s.at[2], rs_r.at[4], mate))
     sent(projr, rs_s.at[2])
-    await_bytes(nrm1, nm_r.at[1])
-    await_bytes(nrm1, nm_s.at[1])
-    nrm[...] = nrm[...] + nrm1[0] + nrm1[1] + nrm1[2]
-    for n, (i, j) in enumerate(plane):
-        launch(remote(nrm, nrm2.at[n], pl_s.at[3], pl_r.at[3], plane_peer("z", "y", i, j)))
-    sent(nrm2, pl_s.at[3])
+    packed_out[...] = dot(pall[mine[0], pl.ds(mine[1], 320), :], packin[...]).astype(BF)
     await_bytes(projr, rs_r.at[4])
     projb[...] = (projp[:, :, c].astype(F32) + projr[...].astype(F32)).astype(BF)
     for n, (i, j) in enumerate(plane):
@@ -475,14 +468,19 @@
             )
         )
     sent(proj1, pl_s.at[4])
+    await_bytes(nrm1, nm_r.at[1])
+    await_bytes(nrm1, nm_s.at[1])
+    nrm[...] = nrm[...] + nrm1[0] + nrm1[1] + nrm1[2]
+    for n, (i, j) in enumerate(plane):
+        launch(remote(nrm, nrm2.at[n], pl_s.at[3], pl_r.at[3], plane_peer("z", "y", i, j)))
+    sent(nrm2, pl_s.at[3])
     for j in range(4):
         conv_take(1, j)
-    for axis in order:
+    for axis in "xzy":
         for j in range(4):
             if conv_axis[0][j] == axis:
                 conv_take(0, j)
         conv_last_send(axis)
-    packed_out[...] = dot(pall[mine[0], pl.ds(mine[1], 320), :], packin[...]).astype(BF)
     await_bytes(nrm2, pl_r.at[3])
     total = nrm[...]
     for n in range(15):
@@ -493,7 +491,7 @@
     for n in range(15):
         total = total + proj1[n].astype(F32)
     gproj_out[...] = total[:, 0:320]
-    for axis in order:
+    for axis in "xzy":
         conv_last_take(axis)
 
     for ref, sem in sends:
@@ -513,7 +511,7 @@
 
 
 def finish(
-    packed_in, gfeat_in, gconv_in, gproj_in, gnorm_in, packed_out, gfeat_out, gconv_out, gproj_out, gnorm_out, sem
+    packed_in, gfeat_in, gconv_in, gproj_in, gnorm_in, packed_out, gfeat_out, gconv_out, gproj_out, gnorm_out, rows, sem
 ):
     copies = [
         pltpu.make_async_copy(packed_in, packed_out, sem.at[0]),
@@ -527,7 +525,9 @@
     for layer in range(2):
         row = gnorm_in[pl.ds(layer * 8 + d // 16, 1), :]
         turned = pltpu.roll(row, LANE - (d % 16) * 8, 1)
-        gnorm_out[layer : layer + 1, :] = turned[:, 0:8]
+        rows[layer : layer + 1, :] = turned[:, 0:8]
+    copies.append(pltpu.make_async_copy(rows, gnorm_out, sem.at[4]))
+    copies[-1].start()
     for one in copies:
         one.wait()
 
@@ -571,8 +571,8 @@
         finish,
         out_shape=tuple(jax.ShapeDtypeStruct(*one) for one in shapes),
         in_specs=[vmem] * 5,
-        out_specs=(hbm, hbm, hbm, hbm, vmem),
-        scratch_shapes=[D((4,))],
+        out_specs=(hbm,) * 5,
+        scratch_shapes=[V((2, 8), F32), D((5,))],
     )(*[pltpu.with_memory_space_constraint(one, pltpu.VMEM) for one in middle])
     return packed.T, gfeat.reshape(32, 32, 512), gconv, gnorm, gproj
 

time: 49.4 us -> 48.9 us (0.990)
  Pallas kernels: 48.7 us -> 48.1 us
    pallas_call x1, Pallas kernels: 1.69 us -> 1.14 us  [local(): pl.pallas_call(finish, out_shape=tuple((jax.ShapeDtypeStruct(*one) for on...]
where the time goes in v5:
time: 48.9 us; the launch traced here: 48.8 us
  Pallas kernels  48.1 us (98%)
  between operations  0.64 us (1%)
    pallas_call x1, Pallas kernels, local(): pl.pallas_call(kernel, out_shape=tuple((pltpu.VMEM(*one) for one in resul...  47 us
    pallas_call x1, Pallas kernels, local(): pl.pallas_call(finish, out_shape=tuple((jax.ShapeDtypeStruct(*one) for on...  1.14 us

profile of v5, /device:TPU:1, one launch (start us, length us, event | category | flops | bytes accessed | tf_op | source)
XLA Modules:
  0.0 48.8 jit_solution(3079217948645089436)
XLA Ops:
  0.6 47.0 %shard_map.128 = (bf16[320,512]{1,0:T(8,128)(2,1)S(1)}, bf16[1024,512]{1,0:T(8,128)(2,1)S(1)}, f32[2,8,512]{2,1,0:T(8,128)S(1)}, f32[16,320]{1,0:T(8,128)S(1)}, f32[16,128]{1,0:T(8,128)S(1)}) custom-call(s32[32]{0:T(128)} %len_hbm.1, s32[32]{0:T(128)} %dest_hbm.1, s32[32]{0:T(128)} %off_hbm.1, f32[2,512]{1,0:T(2,128)} %gain_hbm.1, f32[2,512]{1,0:T(2,128)} %shift_hbm.1, ...), custom_call_target="tpu_custom_call" | custom-call | tf_op jit(solution)/shard_map/pallas_call | solution.py:558
  47.6 1.1 %shard_map.129 = (bf16[320,512]{1,0:T(8,128)(2,1)}, bf16[1024,512]{1,0:T(8,128)(2,1)}, f32[2,8,512]{2,1,0:T(8,128)}, f32[16,320]{1,0:T(8,128)}, f32[2,8]{1,0:T(2,128)}) custom-call(bf16[320,512]{1,0:T(8,128)(2,1)S(1)} %get-tuple-element.15.packed_in, bf16[1024,512]{1,0:T(8,128)(2,1)S(1)} %get-tuple-element.16.gfeat_in, ...), custom_call_target="tpu_custom_call" | custom-call | tf_op jit(solution)/shard_map/pallas_call | solution.py:570

commit v6 on v5

--- a/solution.py
+++ b/solution.py
@@ -241,6 +241,11 @@
         launch(remote(shard(at, own, 160), shard(at, own, 160), ag_s.at[2], ag_r.at[3], mate))
     sent(pall.at[0, pl.ds(0, 480)], ag_s.at[2])
 
+    await_bytes(frecv.at[:, 0], a2a_r.at[0])
+    low, high = pl.ds(0, 16), pl.ds(16, 16)
+    for n, (to, half) in enumerate(((up, low), (down, high), (up, high), (down, low))):
+        launch(remote(frecv.at[half, y], frecv.at[half, y], fg_s.at[0], fg_r.at[min(n, 2)], (dp, to)))
+    sent(frecv.at[low], fg_s.at[0])
     placet[...] = place.T
     for part in range(4):
         slot = (iota((256, 128), 0) >> 3) + part * 32
@@ -249,14 +254,9 @@
         query[part * 256 : part * 256 + 256, :] = (dot(spread, blocks) * 8.0 == column).astype(F32).astype(BF)
     actt[...] = act[...].T
     hidt[...] = hid[...].T
-    await_bytes(pall.at[0, pl.ds(0, 480)], ag_r.at[3])
-    await_bytes(frecv.at[:, 0], a2a_r.at[0])
-    low, high = pl.ds(0, 16), pl.ds(16, 16)
-    for n, (to, half) in enumerate(((up, low), (down, high), (up, high), (down, low))):
-        launch(remote(frecv.at[half, y], frecv.at[half, y], fg_s.at[0], fg_r.at[min(n, 2)], (dp, to)))
-    sent(frecv.at[low], fg_s.at[0])
     await_bytes(gbig, g_r.at[0])
     await_bytes(gsmall, g_r.at[1])
+    await_bytes(pall.at[0, pl.ds(0, 480)], ag_r.at[3])
 
     total = None
     for m in range(2):

time: 48.9 us -> 48.8 us (level)
  no operation moved by 1% of the time
where the time goes in v6:
time: 48.8 us; the launch traced here: 48.7 us
  Pallas kernels  48.1 us (99%)
  between operations  0.64 us (1%)
    pallas_call x1, Pallas kernels, local(): pl.pallas_call(kernel, out_shape=tuple((pltpu.VMEM(*one) for one in resul...  46.9 us
    pallas_call x1, Pallas kernels, local(): pl.pallas_call(finish, out_shape=tuple((jax.ShapeDtypeStruct(*one) for on...  1.14 us

profile of v6, /device:TPU:1, one launch (start us, length us, event | category | flops | bytes accessed | tf_op | source)
XLA Modules:
  0.0 48.7 jit_solution(5668515725978382551)
XLA Ops:
  0.6 46.9 %shard_map.128 = (bf16[320,512]{1,0:T(8,128)(2,1)S(1)}, bf16[1024,512]{1,0:T(8,128)(2,1)S(1)}, f32[2,8,512]{2,1,0:T(8,128)S(1)}, f32[16,320]{1,0:T(8,128)S(1)}, f32[16,128]{1,0:T(8,128)S(1)}) custom-call(s32[32]{0:T(128)} %len_hbm.1, s32[32]{0:T(128)} %dest_hbm.1, s32[32]{0:T(128)} %off_hbm.1, f32[2,512]{1,0:T(2,128)} %gain_hbm.1, f32[2,512]{1,0:T(2,128)} %shift_hbm.1, ...), custom_call_target="tpu_custom_call" | custom-call | tf_op jit(solution)/shard_map/pallas_call | solution.py:558
  47.6 1.1 %shard_map.129 = (bf16[320,512]{1,0:T(8,128)(2,1)}, bf16[1024,512]{1,0:T(8,128)(2,1)}, f32[2,8,512]{2,1,0:T(8,128)}, f32[16,320]{1,0:T(8,128)}, f32[2,8]{1,0:T(2,128)}) custom-call(bf16[320,512]{1,0:T(8,128)(2,1)S(1)} %get-tuple-element.15.packed_in, bf16[1024,512]{1,0:T(8,128)(2,1)S(1)} %get-tuple-element.16.gfeat_in, ...), custom_call_target="tpu_custom_call" | custom-call | tf_op jit(solution)/shard_map/pallas_call | solution.py:570
